TPU v7x, 32 devices: a whole 2x2x4 slice. The times are simulated.
32 devices in a mesh: txt: 4 (over z), clip: 2 (over x), proj: 4 (over y, core).
Axes of the slice: x: 2, y: 2, z: 4, core: 2. Of those that a mesh axis runs over, the one named last changes fastest.
Arguments:
- text_hidden: float32 [1024, 1024], P(('txt', 'clip')), may hold values from -16 to 16
- proj_weight: float32 [1024, 1024], P(None, 'proj'), may hold values from -2 to 2
- clip_embed: float32 [1024, 1024], P(('txt', 'clip'), 'proj'), may hold values from -16 to 16
- positive: int32 [1024], P(('txt', 'clip')), may hold values from 0 to 1023, each once
- logit_scale: float32 [1], replicated, may hold values from 10 to 300
Outputs:
- grad_hidden: float32 [1024, 1024], P(('txt', 'clip'), 'proj')
- grad_weight: float32 [1024, 1024], P(('txt', 'clip'), 'proj')
- grad_clip: float32 [1024, 1024], P(('txt', 'clip'), 'proj')
Inputs may be any that keep to these rules, and one draw needn't show every extreme that they name: `positive`: each clip row is the match of exactly one text row.
All inputs are finite; a program needn't handle non-finite values.
Results may differ from a plain program's by a relative error of at most 0.0003.
Values sent between devices are 32-bit elements; how exact they have to be, the bound alone decides.
No kernel may reach another device: no remote copies, remote signals or barrier semaphores. Data moves between devices by JAX's collectives and lax.ppermute only.
A program may use at most 64 MiB of HBM per device.

v0:
```python
import jax
import jax.numpy as jnp
from jax import lax
from jax.sharding import PartitionSpec as P

EPSILON = 1e-06
PRECISE = lax.Precision.HIGH


def swap(block, *moves):
    axes = tuple(axis for axis, _ in moves)
    sizes = [lax.axis_size(axis) for axis in axes]
    route = []
    total = 1
    for size in sizes:
        total *= size
    for index in range(total):
        rest, coords = index, []
        for size in reversed(sizes):
            coords.insert(0, rest % size)
            rest //= size
        target = 0
        for size, coord, (_, distance) in zip(sizes, coords, moves):
            target = target * size + (coord ^ distance)
        route.append((index, target))
    return lax.ppermute(block, axes if len(axes) > 1 else axes[0], route)


def gather_blocks(block, moves):
    blocks = [block]
    for move in moves:
        if len(blocks) <= 2:
            blocks = blocks + [swap(one, move) for one in blocks]
        else:
            moved = swap(jnp.stack(blocks), move)
            blocks = blocks + [moved[k] for k in range(len(blocks))]
    return blocks


def scatter_blocks(blocks, moves):
    for level in reversed(range(len(moves))):
        half = len(blocks) // 2
        keep, send = blocks[:half], blocks[half:]
        if half <= 2:
            received = [None] * half
            for k in reversed(range(half)):
                received[k] = swap(send[k], moves[level])
        else:
            moved = swap(jnp.stack(send), moves[level])
            received = [moved[k] for k in range(half)]
        blocks = [one + other for one, other in zip(keep, received)]
    return blocks[0]


def dot(a, b, contract):
    return lax.dot_general(
        a, b, ((contract[0], contract[1]), ((), ())), precision=PRECISE, preferred_element_type=jnp.float32
    )


def merge_stats(mine, other):
    top = jnp.maximum(mine[0], other[0])
    total = mine[1] * jnp.exp(mine[0] - top) + other[1] * jnp.exp(other[0] - top)
    return jnp.stack([top, total])


def flip_blocks(stats, q, blocks):
    size = stats.shape[1] // blocks
    order = [k ^ q for k in range(blocks)]
    return jnp.concatenate([stats[:, k * size : (k + 1) * size] for k in order], axis=1)


def body(text_hidden, proj_weight, clip_embed, positive, logit_scale):
    scale = logit_scale[0]
    txt_n, clip_n = lax.axis_size("txt"), lax.axis_size("clip")
    proj_n = lax.axis_size("proj")
    rows = text_hidden.shape[0]
    width = text_hidden.shape[1]
    feat = proj_weight.shape[1]
    groups = txt_n * clip_n
    txt_bits, clip_bits = txt_n.bit_length() - 1, clip_n.bit_length() - 1
    near = ("txt", 1)
    core = ("proj", 1)
    far = ("proj", 2)
    moves = [("txt", 2 << k) for k in range(txt_bits - 1)] + [("clip", 1 << k) for k in range(clip_bits)]
    weights = [d * clip_n if axis == "txt" else d for axis, d in moves]
    count = len(moves)
    blocks = 1 << count
    part = rows // 2

    own_txt, own_clip, own_proj = lax.axis_index("txt"), lax.axis_index("clip"), lax.axis_index("proj")
    own = own_txt * clip_n + own_clip
    own_core = own_proj % 2

    def offset(q):
        return sum(weights[k] for k in range(count) if q >> k & 1)

    clips = gather_blocks(clip_embed, moves)
    clip_keep, clip_send = [], []
    for one in clips:
        clip_keep.append(lax.dynamic_slice_in_dim(one, own_core * part, part))
        clip_send.append(lax.dynamic_slice_in_dim(one, (1 - own_core) * part, part))
    projected = dot(text_hidden, proj_weight, ((1,), (0,)))
    upper = own_txt % 2

    def pair_rows(mine, other):
        whole = jnp.zeros((2 * rows,) + mine.shape[1:], mine.dtype)
        whole = lax.dynamic_update_slice_in_dim(whole, mine, upper * rows, 0)
        return lax.dynamic_update_slice_in_dim(whole, other, (1 - upper) * rows, 0)

    projected_near = swap(projected, near)
    text_raw = pair_rows(projected, projected_near)

    slot = width // groups
    hidden_blocks = text_hidden.reshape(rows, groups, slot)

    def hidden_columns(base):
        return jnp.concatenate(
            [
                lax.dynamic_index_in_dim(hidden_blocks, base ^ offset(q), axis=1, keepdims=False)
                for q in range(blocks)
            ],
            axis=1,
        )

    half_width = blocks * slot
    spare = -(-rows // half_width)
    match_rows = jnp.pad(positive.astype(jnp.float32), (0, spare * half_width - rows)).reshape(spare, half_width)
    hidden_near = swap(jnp.concatenate([hidden_columns(own ^ clip_n), match_rows], axis=0), near)
    hidden_tile = pair_rows(hidden_columns(own), hidden_near[:rows])
    match_near = hidden_near[rows:].reshape(-1)[:rows].astype(jnp.int32)
    matching = jnp.where(upper == 0, jnp.concatenate([positive, match_near]), jnp.concatenate([match_near, positive]))

    cut = blocks - max(blocks // 4, 1)
    half = blocks * part
    keep_tile = jnp.concatenate(clip_keep, axis=0)
    send_tile = jnp.concatenate(clip_send, axis=0)
    squares = [jnp.sum(text_raw * text_raw, axis=1)]
    squares += [jnp.sum(one * one, axis=1) for one in (keep_tile, send_tile)]
    half_rows = -(-half // (2 * rows))

    def as_rows(values):
        size = -(-values.shape[0] // (2 * rows)) * 2 * rows
        return jnp.pad(values, (0, size - values.shape[0])).reshape(-1, 2 * rows)

    squares = [as_rows(one) for one in squares]
    spare_rows = -(-(1 + 2 * half_rows) // 8) * 8

    def with_squares(part_scores, values):
        whole = jnp.zeros((part_scores.shape[0] + spare_rows, 2 * rows), jnp.float32)
        whole = lax.dynamic_update_slice(whole, part_scores, (0, 0))
        return lax.dynamic_update_slice(whole, values, (part_scores.shape[0], 0))

    raw_scores = []
    for k, span in enumerate((slice(0, cut), slice(cut, blocks))):
        keep = jnp.concatenate(clip_keep[span], axis=0)
        send = jnp.concatenate(clip_send[span], axis=0)
        lanes = keep.shape[0]
        part_scores = dot(send, text_raw, ((1,), (1,)))
        if k == 1:
            part_scores = with_squares(part_scores, jnp.concatenate([squares[0], squares[2], squares[1]], axis=0))
        sent = swap(part_scores, core)
        mine = dot(keep, text_raw, ((1,), (1,))) + sent[:lanes]
        if k == 1:
            square_sum = jnp.concatenate(squares, axis=0) + sent[lanes : lanes + 1 + 2 * half_rows]
            mine = with_squares(mine, square_sum)
        mine = mine + swap(mine, far)
        raw_scores.append(mine[:lanes])
    inverse = lax.rsqrt(mine[lanes : lanes + 1 + 2 * half_rows] + EPSILON)
    text_inverse = inverse[0][:, None]
    keep_inverse = inverse[1 : 1 + half_rows].reshape(-1)[:half, None]
    send_inverse = inverse[1 + half_rows :].reshape(-1)[:half, None]
    text_unit = text_raw * text_inverse
    keep_unit = keep_tile * keep_inverse
    send_unit = send_tile * send_inverse
    scores = jnp.concatenate(raw_scores, axis=0) * keep_inverse * (scale * inverse[:1])

    row_max = jnp.max(scores, axis=0)
    col_max = jnp.max(scores, axis=1)
    row_stats = jnp.stack([row_max, jnp.sum(jnp.exp(scores - row_max[None, :]), axis=0)])
    col_stats = jnp.stack([col_max, jnp.sum(jnp.exp(scores - col_max[:, None]), axis=1)])
    row_stats = merge_stats(row_stats, swap(row_stats, core))
    row_stats = merge_stats(row_stats, swap(row_stats, near))
    for k in reversed(range(count)):
        col_stats = merge_stats(col_stats, flip_blocks(swap(col_stats, moves[k]), 1 << k, blocks))

    row_bits, part_bits = rows.bit_length() - 1, part.bit_length() - 1
    relative = lax.shift_right_logical(matching, row_bits) ^ own
    entry = matching & (rows - 1)
    position = entry & (part - 1)
    for k in range(count):
        bit = lax.shift_right_logical(relative, weights[k].bit_length() - 1) & 1
        position = position | (bit << (k + part_bits))
    inside = ((relative >> clip_bits) & 1 == 0) & (entry >> part_bits == own_core)
    column = jnp.where(inside, position, -1)
    matches = (lax.broadcasted_iota(jnp.int32, scores.shape, 0) == column[None, :]).astype(jnp.float32)
    grad = (
        0.5
        * (
            jnp.exp(scores - row_stats[0][None, :]) / row_stats[1][None, :]
            + jnp.exp(scores - col_stats[0][:, None]) / col_stats[1][:, None]
        )
        - matches
    )
    weighted = grad * scores
    along = jnp.concatenate([jnp.sum(weighted, axis=0), jnp.sum(weighted, axis=1)])
    grad_other = swap(grad, core)
    along_other = swap(along, core)
    text_along = (along[: 2 * rows] + along_other[: 2 * rows])[:, None]
    keep_along, send_along = along[2 * rows :, None], along_other[2 * rows :, None]

    text_mine = lax.optimization_barrier(dot(grad, keep_unit, ((0,), (0,))))
    text_parts = []
    for k in range(2):
        cols = slice(k * (feat // 2), (k + 1) * (feat // 2))
        cot = text_mine[:, cols] + dot(grad_other, send_unit[:, cols], ((0,), (0,)))
        text_parts.append((scale * cot - text_unit[:, cols] * text_along) * text_inverse)
    text_back = [one + swap(one, near) for one in text_parts]
    keep_back = (scale * dot(grad, text_unit, ((1,), (0,))) - keep_unit * keep_along) * keep_inverse
    send_back = (scale * dot(grad_other, text_unit, ((1,), (0,))) - send_unit * send_along) * send_inverse
    clip_back = scatter_blocks(
        [
            jnp.concatenate([keep_back[q * part : (q + 1) * part], send_back[q * part : (q + 1) * part]], axis=0)
            for q in range(blocks)
        ],
        moves,
    )
    grad_clip = jnp.where(own_core == 0, clip_back, jnp.concatenate([clip_back[part:], clip_back[:part]], axis=0))

    top = blocks // 2
    outer = [q for q in range(blocks) if q & 1]
    inner = [q for q in range(blocks) if not q & 1]

    def hidden_of(which):
        return jnp.concatenate([hidden_tile[:, q * slot : (q + 1) * slot] for q in which], axis=1)

    halves = []
    for k in range(2):
        crossing = dot(hidden_of(outer), text_back[k], ((0,), (0,)))
        crossing = scatter_blocks([crossing[j * slot : (j + 1) * slot] for j in range(top)], moves[1:])
        halves.append(swap(crossing, moves[0]))
    text_back = jnp.concatenate(text_back, axis=1)
    rest = dot(hidden_of(inner), text_back, ((0,), (0,)))
    rest = scatter_blocks([rest[j * slot : (j + 1) * slot] for j in range(top)], moves[1:])
    grad_weight = rest + jnp.concatenate(halves, axis=1)

    own_back = lax.dynamic_slice_in_dim(text_back, upper * rows, rows)
    hidden_part = dot(own_back, proj_weight, ((1,), (1,)))
    piece = width // proj_n
    hidden_parts = [
        lax.dynamic_slice_in_dim(hidden_part, (own_proj ^ (2 * (q & 1) + (q >> 1))) * piece, piece, axis=1)
        for q in range(proj_n)
    ]
    grad_hidden = scatter_blocks(hidden_parts, [far, core])
    return (grad_hidden, grad_weight, grad_clip)


def solution(mesh):
    in_specs = (
        P(("txt", "clip"), None),
        P(None, "proj"),
        P(("txt", "clip"), "proj"),
        P(("txt", "clip")),
        P(),
    )
    out_specs = (P(("txt", "clip"), "proj"), P(("txt", "clip"), "proj"), P(("txt", "clip"), "proj"))
    return jax.shard_map(body, mesh=mesh, in_specs=in_specs, out_specs=out_specs, check_vma=False)
```

profile of v0, /device:TPU:0, one launch (start us, length us, event | category | flops | bytes accessed | tf_op | source)
XLA Modules:
  0.0 75.7 jit_solution(9944880364646645661)
XLA Ops:
  0.6 4.1 %collective-permute-start = (f32[128,256]{1,0:T(8,128)}, f32[128,256]{1,0:T(8,128)S(1)}, u32[]{:S(2)}, u32[]{:S(2)}) collective-permute-start(f32[128,256]{1,0:T(8,128)} %param.7), channel_id=1, source_target_pairs={{0,16},{8,24},{16,0},{24,8},{1,17},{9,25},{17,1},{25,9},{2,18},{10... | collective-permute-start | bytes 393224 | tf_op jit(solution)/shard_map/ppermute | solution.py:26
  4.8 1.5 %collective-permute-start.1 = (f32[128,256]{1,0:T(8,128)}, f32[128,256]{1,0:T(8,128)S(1)}, u32[]{:S(2)}, u32[]{:S(2)}) collective-permute-start(f32[128,256]{1,0:T(8,128)} %param.7), channel_id=1, source_target_pairs={{0,4},{4,0},{1,5},{5,1},{2,6},{6,2},{3,7},{7,3},{8,12},{12,8},{9,1... | collective-permute-start | bytes 393224 | tf_op jit(solution)/shard_map/ppermute | solution.py:26
  6.3 1.5 %constant_dynamic-update-slice_fusion.1 = (f32[256,256]{1,0:T(8,128)S(1)}, f32[128,256]{1,0:T(8,128)S(1)}) fusion(f32[256,256]{1,0:T(8,128)S(1)} %broadcast_in_dim.8, s32[]{:T(128)S(6)} %select_n.100, f32[128,1024]{1,0:T(8,128)} %param.5, f32[1024,256]{1,0:T(8,128)S(1)} %copy-done), kind=kOutput, calls=%fused_computation.92 | convolution fusion | flops 201326592 | bytes 1835012 | tf_op jit(solution)/shard_map/dot_general | solution.py:56
  7.8 1.6 %collective-permute-start.2 = (f32[128,256]{1,0:T(8,128)S(1)}, f32[128,256]{1,0:T(8,128)S(1)}, u32[]{:S(2)}, u32[]{:S(2)}) collective-permute-start(f32[128,256]{1,0:T(8,128)S(1)} %get-tuple-element.65), channel_id=1, source_target_pairs={{0,8},{8,0},{16,24},{24,16},{1,9},{9,1},{17,25},{25,17},{2,10},{10... | collective-permute-start | bytes 393224 | tf_op jit(solution)/shard_map/ppermute | solution.py:26
  9.5 0.7 copy-done.9
  10.7 0.5 collective-permute-start.12
  11.3 0.8 %copy-done.2 = f32[128,256]{1,0:T(8,128)S(1)} copy-done((f32[128,256]{1,0:T(8,128)S(1)}, f32[128,256]{1,0:T(8,128)}, u32[]{:S(2)}) %copy-start.2) | copy-done | bytes 131096
  12.9 0.6 collective-permute-start.5
  13.5 0.7 collective-permute-done.2
  14.8 3.1 %collective-permute-done.5 = f32[128,256]{1,0:T(8,128)S(1)} collective-permute-done((f32[128,256]{1,0:T(8,128)S(1)}, f32[128,256]{1,0:T(8,128)S(1)}, u32[]{:S(2)}, u32[]{:S(2)}) %collective-permute-start.5) | collective-permute-done | bytes 131104 | tf_op jit(solution)/shard_map/ppermute | solution.py:26
  18.2 0.6 dynamic_update_slice.26
  19.1 0.5 copy-done.5
  19.6 1.3 %dynamic_update_slice.27 = f32[72,256]{1,0:T(8,128)} dynamic-update-slice(f32[72,256]{1,0:T(8,128)} %dynamic_update_slice.26, f32[3,256]{1,0:T(4,128)S(1)} %fusion.38, s32[]{:T(128)} %constant.70.clone.1, s32[]{:T(128)} %constant.67.clone.1) | dynamic-update-slice | bytes 6148 | tf_op jit(solution)/shard_map/dynamic_update_slice | solution.py:152
  21.1 0.6 copy-done.10
  21.7 0.7 collective-permute-done.6
  22.8 0.6 copy-done.4
  23.6 1.6 %collective-permute-start.7 = (f32[72,256]{1,0:T(8,128)S(1)}, f32[72,256]{1,0:T(8,128)S(1)}, u32[]{:S(2)}, u32[]{:S(2)}) collective-permute-start(f32[72,256]{1,0:T(8,128)S(1)} %dynamic_update_slice.29), channel_id=1, source_target_pairs={{0,2},{1,3},{2,0},{3,1},{4,6},{5,7},{6,4},{7,5},{8,10},{9,11},{10,... | collective-permute-start | bytes 221192 | tf_op jit(solution)/shard_map/ppermute | solution.py:26
  25.5 0.6 collective-permute-start.4
  26.1 1.9 %collective-permute-done.7 = f32[72,256]{1,0:T(8,128)S(1)} collective-permute-done((f32[72,256]{1,0:T(8,128)S(1)}, f32[72,256]{1,0:T(8,128)S(1)}, u32[]{:S(2)}, u32[]{:S(2)}) %collective-permute-start.7) | collective-permute-done | bytes 73760 | tf_op jit(solution)/shard_map/ppermute | solution.py:26
  28.3 4.0 %collective-permute-done.4 = f32[192,256]{1,0:T(8,128)S(1)} collective-permute-done((f32[192,256]{1,0:T(8,128)S(1)}, f32[192,256]{1,0:T(8,128)S(1)}, u32[]{:S(2)}, u32[]{:S(2)}) %collective-permute-start.4) | collective-permute-done | bytes 196640 | tf_op jit(solution)/shard_map/ppermute | solution.py:26
  32.8 0.6 collective-permute-start.10
  33.5 3.0 %collective-permute-done.10 = f32[2,256]{1,0:T(2,128)S(1)} collective-permute-done((f32[2,256]{1,0:T(2,128)S(1)}, f32[2,256]{1,0:T(2,128)S(1)}, u32[]{:S(2)}, u32[]{:S(2)}) %collective-permute-start.10) | collective-permute-done | bytes 2080 | tf_op jit(solution)/shard_map/ppermute | solution.py:26
  37.0 2.7 %collective-permute-start.9 = (f32[2,256]{1,0:T(2,128)S(1)}, f32[2,256]{1,0:T(2,128)S(1)}, u32[]{:S(2)}, u32[]{:S(2)}) collective-permute-start(f32[2,256]{1,0:T(2,128)S(1)} %pad_maximum_fusion.14), channel_id=1, source_target_pairs={{0,8},{8,0},{16,24},{24,16},{1,9},{9,1},{17,25},{25,17},{2,10},{10... | collective-permute-start | bytes 6152 | tf_op jit(solution)/shard_map/ppermute | solution.py:26
  39.7 1.4 %collective-permute-done.11 = f32[2,256]{1,0:T(2,128)S(1)} collective-permute-done((f32[2,256]{1,0:T(2,128)S(1)}, f32[2,256]{1,0:T(2,128)S(1)}, u32[]{:S(2)}, u32[]{:S(2)}) %collective-permute-start.11) | collective-permute-done | bytes 2080 | tf_op jit(solution)/shard_map/ppermute | solution.py:26
  41.6 0.5 fusion.13
  42.1 0.5 collective-permute-start.14
  42.9 0.7 collective-permute-done.14
  44.4 2.1 %collective-permute-start.15 = (f32[256,128]{1,0:T(8,128)S(1)}, f32[256,128]{1,0:T(8,128)S(1)}, u32[]{:S(2)}, u32[]{:S(2)}) collective-permute-start(f32[256,128]{1,0:T(8,128)S(1)} %fusion.7), channel_id=1, source_target_pairs={{0,8},{8,0},{16,24},{24,16},{1,9},{9,1},{17,25},{25,17},{2,10},{10... | collective-permute-start | bytes 393224 | tf_op jit(solution)/shard_map/ppermute | solution.py:26
  47.0 1.5 %collective-permute-start.25 = (f32[128,256]{1,0:T(8,128)S(1)}, f32[128,256]{1,0:T(8,128)S(1)}, u32[]{:S(2)}, u32[]{:S(2)}) collective-permute-start(f32[128,256]{1,0:T(8,128)S(1)} %pad_maximum_fusion.8), channel_id=1, source_target_pairs={{0,4},{4,0},{1,5},{5,1},{2,6},{6,2},{3,7},{7,3},{8,12},{12,8},{9,1... | collective-permute-start | bytes 393224 | tf_op jit(solution)/shard_map/ppermute | solution.py:26
  48.5 0.6 collective-permute-start.26
  49.1 1.7 %collective-permute-done.15 = f32[256,128]{1,0:T(8,128)S(1)} collective-permute-done((f32[256,128]{1,0:T(8,128)S(1)}, f32[256,128]{1,0:T(8,128)S(1)}, u32[]{:S(2)}, u32[]{:S(2)}) %collective-permute-start.15) | collective-permute-done | bytes 131104 | tf_op jit(solution)/shard_map/ppermute | solution.py:26
  50.8 2.2 %collective-permute-done.16 = f32[256,128]{1,0:T(8,128)S(1)} collective-permute-done((f32[256,128]{1,0:T(8,128)S(1)}, f32[256,128]{1,0:T(8,128)S(1)}, u32[]{:S(2)}, u32[]{:S(2)}) %collective-permute-start.16) | collective-permute-done | bytes 131104 | tf_op jit(solution)/shard_map/ppermute | solution.py:26
  53.1 0.7 fusion.30
  54.5 0.6 collective-permute-done.26
  55.1 1.7 %collective-permute-start.27 = (f32[128,256]{1,0:T(8,128)S(1)}, f32[128,256]{1,0:T(8,128)S(1)}, u32[]{:S(2)}, u32[]{:S(2)}) collective-permute-start(f32[128,256]{1,0:T(8,128)S(1)} %maximum_add_fusion.1), channel_id=1, source_target_pairs={{0,16},{8,24},{16,0},{24,8},{1,17},{9,25},{17,1},{25,9},{2,18},{10... | collective-permute-start | bytes 393224 | tf_op jit(solution)/shard_map/ppermute | solution.py:26
  57.0 0.5 collective-permute-start.18
  57.5 0.9 %collective-permute-start.21 = (f32[128,128]{1,0:T(8,128)S(1)}, f32[128,128]{1,0:T(8,128)S(1)}, u32[]{:S(2)}, u32[]{:S(2)}) collective-permute-start(f32[128,128]{1,0:T(8,128)S(1)} %slice.254), channel_id=1, source_target_pairs={{0,4},{4,0},{1,5},{5,1},{2,6},{6,2},{3,7},{7,3},{8,12},{12,8},{9,1... | collective-permute-start | bytes 196616 | tf_op jit(solution)/shard_map/ppermute | solution.py:26
  58.8 3.0 %collective-permute-done.21 = f32[128,128]{1,0:T(8,128)S(1)} collective-permute-done((f32[128,128]{1,0:T(8,128)S(1)}, f32[128,128]{1,0:T(8,128)S(1)}, u32[]{:S(2)}, u32[]{:S(2)}) %collective-permute-start.21) | collective-permute-done | bytes 65568 | tf_op jit(solution)/shard_map/ppermute | solution.py:26
  61.8 0.8 %collective-permute-start.23 = (f32[128,128]{1,0:T(8,128)S(1)}, f32[128,128]{1,0:T(8,128)S(1)}, u32[]{:S(2)}, u32[]{:S(2)}) collective-permute-start(f32[128,128]{1,0:T(8,128)S(1)} %slice.256), channel_id=1, source_target_pairs={{0,4},{4,0},{1,5},{5,1},{2,6},{6,2},{3,7},{7,3},{8,12},{12,8},{9,1... | collective-permute-start | bytes 196616 | tf_op jit(solution)/shard_map/ppermute | solution.py:26
  62.6 3.4 %collective-permute-done.23 = f32[128,128]{1,0:T(8,128)S(1)} collective-permute-done((f32[128,128]{1,0:T(8,128)S(1)}, f32[128,128]{1,0:T(8,128)S(1)}, u32[]{:S(2)}, u32[]{:S(2)}) %collective-permute-start.23) | collective-permute-done | bytes 65568 | tf_op jit(solution)/shard_map/ppermute | solution.py:26
  66.1 0.8 %collective-permute-start.20 = (f32[128,256]{1,0:T(8,128)S(1)}, f32[128,256]{1,0:T(8,128)S(1)}, u32[]{:S(2)}, u32[]{:S(2)}) collective-permute-start(f32[128,256]{1,0:T(8,128)S(1)} %slice.250), channel_id=1, source_target_pairs={{0,4},{4,0},{1,5},{5,1},{2,6},{6,2},{3,7},{7,3},{8,12},{12,8},{9,1... | collective-permute-start | bytes 393224 | tf_op jit(solution)/shard_map/ppermute | solution.py:26
  66.9 2.0 %collective-permute-start.22 = (f32[128,128]{1,0:T(8,128)S(1)}, f32[128,128]{1,0:T(8,128)S(1)}, u32[]{:S(2)}, u32[]{:S(2)}) collective-permute-start(f32[128,128]{1,0:T(8,128)S(1)} %slice_add_fusion.2), channel_id=1, source_target_pairs={{0,16},{8,24},{16,0},{24,8},{1,17},{9,25},{17,1},{25,9},{2,18},{10... | collective-permute-start | bytes 196616 | tf_op jit(solution)/shard_map/ppermute | solution.py:26
  68.9 1.0 %collective-permute-start.24 = (f32[128,128]{1,0:T(8,128)S(1)}, f32[128,128]{1,0:T(8,128)S(1)}, u32[]{:S(2)}, u32[]{:S(2)}) collective-permute-start(f32[128,128]{1,0:T(8,128)S(1)} %slice_add_fusion.1), channel_id=1, source_target_pairs={{0,16},{8,24},{16,0},{24,8},{1,17},{9,25},{17,1},{25,9},{2,18},{10... | collective-permute-start | bytes 196616 | tf_op jit(solution)/shard_map/ppermute | solution.py:26
  70.0 1.5 %collective-permute-start.19 = (f32[128,256]{1,0:T(8,128)S(1)}, f32[128,256]{1,0:T(8,128)S(1)}, u32[]{:S(2)}, u32[]{:S(2)}) collective-permute-start(f32[128,256]{1,0:T(8,128)S(1)} %dynamic-slice_add_fusion), channel_id=1, source_target_pairs={{0,2},{1,3},{2,0},{3,1},{4,6},{5,7},{6,4},{7,5},{8,10},{9,11},{10,... | collective-permute-start | bytes 393224 | tf_op jit(solution)/shard_map/ppermute | solution.py:26
  71.5 0.7 maximum_select_fusion
  72.5 1.6 %collective-permute-done.24 = f32[128,128]{1,0:T(8,128)S(1)} collective-permute-done((f32[128,128]{1,0:T(8,128)S(1)}, f32[128,128]{1,0:T(8,128)S(1)}, u32[]{:S(2)}, u32[]{:S(2)}) %collective-permute-start.24) | collective-permute-done | bytes 65568 | tf_op jit(solution)/shard_map/ppermute | solution.py:26
  74.1 0.7 fusion.32
  75.0 0.7 add_add_fusion
  (113 shorter events, 7.8 us)
Async XLA Ops:
  0.6 5.7 %copy-start = (f32[1024,256]{1,0:T(8,128)S(1)}, f32[1024,256]{1,0:T(8,128)}, u32[]{:S(2)}) copy-start(f32[1024,256]{1,0:T(8,128)} %param.6) | copy-start | bytes 3145732
  0.6 12.2 %collective-permute-start = (f32[128,256]{1,0:T(8,128)}, f32[128,256]{1,0:T(8,128)S(1)}, u32[]{:S(2)}, u32[]{:S(2)}) collective-permute-start(f32[128,256]{1,0:T(8,128)} %param.7), channel_id=1, source_target_pairs={{0,16},{8,24},{16,0},{24,8},{1,17},{9,25},{17,1},{25,9},{2,18},{10... | collective-permute-start | bytes 393224 | tf_op jit(solution)/shard_map/ppermute | solution.py:26
  4.8 8.7 %collective-permute-start.1 = (f32[128,256]{1,0:T(8,128)}, f32[128,256]{1,0:T(8,128)S(1)}, u32[]{:S(2)}, u32[]{:S(2)}) collective-permute-start(f32[128,256]{1,0:T(8,128)} %param.7), channel_id=1, source_target_pairs={{0,4},{4,0},{1,5},{5,1},{2,6},{6,2},{3,7},{7,3},{8,12},{12,8},{9,1... | collective-permute-start | bytes 393224 | tf_op jit(solution)/shard_map/ppermute | solution.py:26
  6.3 3.8 %copy-start.1 = (f32[128,1024]{1,0:T(8,128)S(1)}, f32[128,1024]{1,0:T(8,128)}, u32[]{:S(2)}) copy-start(f32[128,1024]{1,0:T(8,128)} %param.5) | copy-start | bytes 1572868
  7.8 6.4 %collective-permute-start.2 = (f32[128,256]{1,0:T(8,128)S(1)}, f32[128,256]{1,0:T(8,128)S(1)}, u32[]{:S(2)}, u32[]{:S(2)}) collective-permute-start(f32[128,256]{1,0:T(8,128)S(1)} %get-tuple-element.65), channel_id=1, source_target_pairs={{0,8},{8,0},{16,24},{24,16},{1,9},{9,1},{17,25},{25,17},{2,10},{10... | collective-permute-start | bytes 393224 | tf_op jit(solution)/shard_map/ppermute | solution.py:26
  9.5 0.7 copy-start.9
  10.7 10.3 %collective-permute-start.12 = (f32[129,512]{1,0:T(8,128)S(1)}, f32[129,512]{1,0:T(8,128)S(1)}, u32[]{:S(2)}, u32[]{:S(2)}) collective-permute-start(f32[129,512]{1,0:T(8,128)S(1)} %pad_maximum_fusion.1), channel_id=1, source_target_pairs={{0,8},{8,0},{16,24},{24,16},{1,9},{9,1},{17,25},{25,17},{2,10},{10... | collective-permute-start | bytes 792584 | tf_op jit(solution)/shard_map/ppermute | solution.py:26
  11.3 0.9 %copy-start.2 = (f32[128,256]{1,0:T(8,128)S(1)}, f32[128,256]{1,0:T(8,128)}, u32[]{:S(2)}) copy-start(f32[128,256]{1,0:T(8,128)} %param.7) | copy-start | bytes 393220
  12.9 5.0 %collective-permute-start.5 = (f32[128,256]{1,0:T(8,128)S(1)}, f32[128,256]{1,0:T(8,128)S(1)}, u32[]{:S(2)}, u32[]{:S(2)}) collective-permute-start(f32[128,256]{1,0:T(8,128)S(1)} %collective-permute-done), channel_id=1, source_target_pairs={{0,4},{4,0},{1,5},{5,1},{2,6},{6,2},{3,7},{7,3},{8,12},{12,8},{9,1... | collective-permute-start | bytes 393224 | tf_op jit(solution)/shard_map/ppermute | solution.py:26
  14.6 10.6 %collective-permute-start.3 = (f32[192,256]{1,0:T(8,128)S(1)}, f32[192,256]{1,0:T(8,128)S(1)}, u32[]{:S(2)}, u32[]{:S(2)}) collective-permute-start(f32[192,256]{1,0:T(8,128)S(1)} %fusion.22), channel_id=1, source_target_pairs={{0,1},{1,0},{2,3},{3,2},{4,5},{5,4},{6,7},{7,6},{8,9},{9,8},{10,11... | collective-permute-start | bytes 589832 | tf_op jit(solution)/shard_map/ppermute | solution.py:26
  14.8 4.2 %copy-start.3 = (f32[256]{0:T(256)}, f32[256]{0:T(256)S(1)}, u32[]{:S(2)}) copy-start(f32[256]{0:T(256)S(1)} %multiply_reduce_fusion.2) | copy-start | bytes 3076
  19.0 0.6 copy-start.5
  19.0 0.6 copy-start.7
  21.0 1.5 %collective-permute-start.6 = (f32[72,256]{1,0:T(8,128)}, f32[72,256]{1,0:T(8,128)S(1)}, u32[]{:S(2)}, u32[]{:S(2)}) collective-permute-start(f32[72,256]{1,0:T(8,128)} %dynamic_update_slice.27), channel_id=1, source_target_pairs={{0,1},{1,0},{2,3},{3,2},{4,5},{5,4},{6,7},{7,6},{8,9},{9,8},{10,11... | collective-permute-start | bytes 221192 | tf_op jit(solution)/shard_map/ppermute | solution.py:26
  21.0 0.7 copy-start.10
  22.7 0.7 copy-start.4
  22.7 0.7 copy-start.6
  22.7 0.7 copy-start.8
  23.6 4.4 %collective-permute-start.7 = (f32[72,256]{1,0:T(8,128)S(1)}, f32[72,256]{1,0:T(8,128)S(1)}, u32[]{:S(2)}, u32[]{:S(2)}) collective-permute-start(f32[72,256]{1,0:T(8,128)S(1)} %dynamic_update_slice.29), channel_id=1, source_target_pairs={{0,2},{1,3},{2,0},{3,1},{4,6},{5,7},{6,4},{7,5},{8,10},{9,11},{10,... | collective-permute-start | bytes 221192 | tf_op jit(solution)/shard_map/ppermute | solution.py:26
  25.5 6.7 %collective-permute-start.4 = (f32[192,256]{1,0:T(8,128)S(1)}, f32[192,256]{1,0:T(8,128)S(1)}, u32[]{:S(2)}, u32[]{:S(2)}) collective-permute-start(f32[192,256]{1,0:T(8,128)S(1)} %convolution_add_fusion), channel_id=1, source_target_pairs={{0,2},{1,3},{2,0},{3,1},{4,6},{5,7},{6,4},{7,5},{8,10},{9,11},{10,... | collective-permute-start | bytes 589832 | tf_op jit(solution)/shard_map/ppermute | solution.py:26
  32.8 3.7 %collective-permute-start.10 = (f32[2,256]{1,0:T(2,128)S(1)}, f32[2,256]{1,0:T(2,128)S(1)}, u32[]{:S(2)}, u32[]{:S(2)}) collective-permute-start(f32[2,256]{1,0:T(2,128)S(1)} %pad_maximum_fusion.15), channel_id=1, source_target_pairs={{0,4},{4,0},{1,5},{5,1},{2,6},{6,2},{3,7},{7,3},{8,12},{12,8},{9,1... | collective-permute-start | bytes 6152 | tf_op jit(solution)/shard_map/ppermute | solution.py:26
  33.4 3.5 %collective-permute-start.8 = (f32[2,256]{1,0:T(2,128)S(1)}, f32[2,256]{1,0:T(2,128)S(1)}, u32[]{:S(2)}, u32[]{:S(2)}) collective-permute-start(f32[2,256]{1,0:T(2,128)S(1)} %pad_maximum_fusion.13), channel_id=1, source_target_pairs={{0,1},{1,0},{2,3},{3,2},{4,5},{5,4},{6,7},{7,6},{8,9},{9,8},{10,11... | collective-permute-start | bytes 6152 | tf_op jit(solution)/shard_map/ppermute | solution.py:26
  36.5 4.5 %collective-permute-start.11 = (f32[2,256]{1,0:T(2,128)S(1)}, f32[2,256]{1,0:T(2,128)S(1)}, u32[]{:S(2)}, u32[]{:S(2)}) collective-permute-start(f32[2,256]{1,0:T(2,128)S(1)} %pad_maximum_fusion.16), channel_id=1, source_target_pairs={{0,16},{8,24},{16,0},{24,8},{1,17},{9,25},{17,1},{25,9},{2,18},{10... | collective-permute-start | bytes 6152 | tf_op jit(solution)/shard_map/ppermute | solution.py:26
  37.0 4.3 %collective-permute-start.9 = (f32[2,256]{1,0:T(2,128)S(1)}, f32[2,256]{1,0:T(2,128)S(1)}, u32[]{:S(2)}, u32[]{:S(2)}) collective-permute-start(f32[2,256]{1,0:T(2,128)S(1)} %pad_maximum_fusion.14), channel_id=1, source_target_pairs={{0,8},{8,0},{16,24},{24,16},{1,9},{9,1},{17,25},{25,17},{2,10},{10... | collective-permute-start | bytes 6152 | tf_op jit(solution)/shard_map/ppermute | solution.py:26
  42.1 1.6 %collective-permute-start.13 = (f32[256,256]{1,0:T(8,128)S(1)}, f32[256,256]{1,0:T(8,128)S(1)}, u32[]{:S(2)}, u32[]{:S(2)}) collective-permute-start(f32[256,256]{1,0:T(8,128)S(1)} %get-tuple-element.7), channel_id=1, source_target_pairs={{0,1},{1,0},{2,3},{3,2},{4,5},{5,4},{6,7},{7,6},{8,9},{9,8},{10,11... | collective-permute-start | bytes 786440 | tf_op jit(solution)/shard_map/ppermute | solution.py:26
  42.1 1.5 %collective-permute-start.14 = (f32[512]{0:T(512)S(1)}, f32[512]{0:T(512)S(1)}, u32[]{:S(2)}, u32[]{:S(2)}) collective-permute-start(f32[512]{0:T(512)S(1)} %pad_maximum_fusion.18), channel_id=1, source_target_pairs={{0,1},{1,0},{2,3},{3,2},{4,5},{5,4},{6,7},{7,6},{8,9},{9,8},{10,11... | collective-permute-start | bytes 6152 | tf_op jit(solution)/shard_map/ppermute | solution.py:26
  44.4 6.4 %collective-permute-start.15 = (f32[256,128]{1,0:T(8,128)S(1)}, f32[256,128]{1,0:T(8,128)S(1)}, u32[]{:S(2)}, u32[]{:S(2)}) collective-permute-start(f32[256,128]{1,0:T(8,128)S(1)} %fusion.7), channel_id=1, source_target_pairs={{0,8},{8,0},{16,24},{24,16},{1,9},{9,1},{17,25},{25,17},{2,10},{10... | collective-permute-start | bytes 393224 | tf_op jit(solution)/shard_map/ppermute | solution.py:26
  46.9 6.2 %collective-permute-start.16 = (f32[256,128]{1,0:T(8,128)S(1)}, f32[256,128]{1,0:T(8,128)S(1)}, u32[]{:S(2)}, u32[]{:S(2)}) collective-permute-start(f32[256,128]{1,0:T(8,128)S(1)} %fusion.4), channel_id=1, source_target_pairs={{0,8},{8,0},{16,24},{24,16},{1,9},{9,1},{17,25},{25,17},{2,10},{10... | collective-permute-start | bytes 393224 | tf_op jit(solution)/shard_map/ppermute | solution.py:26
  47.0 19.9 %collective-permute-start.25 = (f32[128,256]{1,0:T(8,128)S(1)}, f32[128,256]{1,0:T(8,128)S(1)}, u32[]{:S(2)}, u32[]{:S(2)}) collective-permute-start(f32[128,256]{1,0:T(8,128)S(1)} %pad_maximum_fusion.8), channel_id=1, source_target_pairs={{0,4},{4,0},{1,5},{5,1},{2,6},{6,2},{3,7},{7,3},{8,12},{12,8},{9,1... | collective-permute-start | bytes 393224 | tf_op jit(solution)/shard_map/ppermute | solution.py:26
  48.5 6.6 %collective-permute-start.26 = (f32[128,256]{1,0:T(8,128)S(1)}, f32[128,256]{1,0:T(8,128)S(1)}, u32[]{:S(2)}, u32[]{:S(2)}) collective-permute-start(f32[128,256]{1,0:T(8,128)S(1)} %pad_maximum_fusion.9), channel_id=1, source_target_pairs={{0,4},{4,0},{1,5},{5,1},{2,6},{6,2},{3,7},{7,3},{8,12},{12,8},{9,1... | collective-permute-start | bytes 393224 | tf_op jit(solution)/shard_map/ppermute | solution.py:26
  55.1 13.8 %collective-permute-start.27 = (f32[128,256]{1,0:T(8,128)S(1)}, f32[128,256]{1,0:T(8,128)S(1)}, u32[]{:S(2)}, u32[]{:S(2)}) collective-permute-start(f32[128,256]{1,0:T(8,128)S(1)} %maximum_add_fusion.1), channel_id=1, source_target_pairs={{0,16},{8,24},{16,0},{24,8},{1,17},{9,25},{17,1},{25,9},{2,18},{10... | collective-permute-start | bytes 393224 | tf_op jit(solution)/shard_map/ppermute | solution.py:26
  56.9 17.9 %collective-permute-start.17 = (f32[128,256]{1,0:T(8,128)S(1)}, f32[128,256]{1,0:T(8,128)S(1)}, u32[]{:S(2)}, u32[]{:S(2)}) collective-permute-start(f32[128,256]{1,0:T(8,128)S(1)} %get-tuple-element.28), channel_id=1, source_target_pairs={{0,1},{1,0},{2,3},{3,2},{4,5},{5,4},{6,7},{7,6},{8,9},{9,8},{10,11... | collective-permute-start | bytes 393224 | tf_op jit(solution)/shard_map/ppermute | solution.py:26
  57.0 13.0 %collective-permute-start.18 = (f32[128,256]{1,0:T(8,128)S(1)}, f32[128,256]{1,0:T(8,128)S(1)}, u32[]{:S(2)}, u32[]{:S(2)}) collective-permute-start(f32[128,256]{1,0:T(8,128)S(1)} %get-tuple-element.29), channel_id=1, source_target_pairs={{0,1},{1,0},{2,3},{3,2},{4,5},{5,4},{6,7},{7,6},{8,9},{9,8},{10,11... | collective-permute-start | bytes 393224 | tf_op jit(solution)/shard_map/ppermute | solution.py:26
  57.5 4.3 %collective-permute-start.21 = (f32[128,128]{1,0:T(8,128)S(1)}, f32[128,128]{1,0:T(8,128)S(1)}, u32[]{:S(2)}, u32[]{:S(2)}) collective-permute-start(f32[128,128]{1,0:T(8,128)S(1)} %slice.254), channel_id=1, source_target_pairs={{0,4},{4,0},{1,5},{5,1},{2,6},{6,2},{3,7},{7,3},{8,12},{12,8},{9,1... | collective-permute-start | bytes 196616 | tf_op jit(solution)/shard_map/ppermute | solution.py:26
  61.8 4.3 %collective-permute-start.23 = (f32[128,128]{1,0:T(8,128)S(1)}, f32[128,128]{1,0:T(8,128)S(1)}, u32[]{:S(2)}, u32[]{:S(2)}) collective-permute-start(f32[128,128]{1,0:T(8,128)S(1)} %slice.256), channel_id=1, source_target_pairs={{0,4},{4,0},{1,5},{5,1},{2,6},{6,2},{3,7},{7,3},{8,12},{12,8},{9,1... | collective-permute-start | bytes 196616 | tf_op jit(solution)/shard_map/ppermute | solution.py:26
  66.1 6.1 %collective-permute-start.20 = (f32[128,256]{1,0:T(8,128)S(1)}, f32[128,256]{1,0:T(8,128)S(1)}, u32[]{:S(2)}, u32[]{:S(2)}) collective-permute-start(f32[128,256]{1,0:T(8,128)S(1)} %slice.250), channel_id=1, source_target_pairs={{0,4},{4,0},{1,5},{5,1},{2,6},{6,2},{3,7},{7,3},{8,12},{12,8},{9,1... | collective-permute-start | bytes 393224 | tf_op jit(solution)/shard_map/ppermute | solution.py:26
  66.9 5.6 %collective-permute-start.22 = (f32[128,128]{1,0:T(8,128)S(1)}, f32[128,128]{1,0:T(8,128)S(1)}, u32[]{:S(2)}, u32[]{:S(2)}) collective-permute-start(f32[128,128]{1,0:T(8,128)S(1)} %slice_add_fusion.2), channel_id=1, source_target_pairs={{0,16},{8,24},{16,0},{24,8},{1,17},{9,25},{17,1},{25,9},{2,18},{10... | collective-permute-start | bytes 196616 | tf_op jit(solution)/shard_map/ppermute | solution.py:26
  68.9 5.2 %collective-permute-start.24 = (f32[128,128]{1,0:T(8,128)S(1)}, f32[128,128]{1,0:T(8,128)S(1)}, u32[]{:S(2)}, u32[]{:S(2)}) collective-permute-start(f32[128,128]{1,0:T(8,128)S(1)} %slice_add_fusion.1), channel_id=1, source_target_pairs={{0,16},{8,24},{16,0},{24,8},{1,17},{9,25},{17,1},{25,9},{2,18},{10... | collective-permute-start | bytes 196616 | tf_op jit(solution)/shard_map/ppermute | solution.py:26
  70.0 5.0 %collective-permute-start.19 = (f32[128,256]{1,0:T(8,128)S(1)}, f32[128,256]{1,0:T(8,128)S(1)}, u32[]{:S(2)}, u32[]{:S(2)}) collective-permute-start(f32[128,256]{1,0:T(8,128)S(1)} %dynamic-slice_add_fusion), channel_id=1, source_target_pairs={{0,2},{1,3},{2,0},{3,1},{4,6},{5,7},{6,4},{7,5},{8,10},{9,11},{10,... | collective-permute-start | bytes 393224 | tf_op jit(solution)/shard_map/ppermute | solution.py:26
where the time goes:
time: 75.9 us; the launch traced here: 75.7 us
  waiting for transfers between devices  28.7 us (38%)
  starting transfers between devices  28.5 us (38%)
  matrix products  6.36 us (8%)
  local copies, waits for them, and re-layouts  6.33 us (8%)
  other arithmetic  3.79 us (5%)
  between operations  1.94 us (3%)
    ppermute x28, waiting for transfers between devices, swap(): return lax.ppermute(block, axes if len(axes) > 1 else axes[0], route)  28.7 us
    ppermute x28, starting transfers between devices, swap(): return lax.ppermute(block, axes if len(axes) > 1 else axes[0], route)  28.5 us
    dot_general x14, matrix products, dot(): lax.dot_general(a, b, ((contract[0], contract[1]), ((), ())), precision=P...  6.36 us
    unnamed x23, local copies, waits for them, and re-layouts  3.48 us
  transfers between devices with their start and end apart: 28, of which 16 were waited for; matrix products, arithmetic and copies ran while one was open for 14% of the time, Pallas kernels for 0%

commit v1 on v0

--- a/solution.py
+++ b/solution.py
@@ -146,10 +146,10 @@
     squares = [as_rows(one) for one in squares]
     spare_rows = -(-(1 + 2 * half_rows) // 8) * 8
 
-    def with_squares(part_scores, values):
-        whole = jnp.zeros((part_scores.shape[0] + spare_rows, 2 * rows), jnp.float32)
-        whole = lax.dynamic_update_slice(whole, part_scores, (0, 0))
-        return lax.dynamic_update_slice(whole, values, (part_scores.shape[0], 0))
+    def with_rows(block, values):
+        whole = jnp.zeros((block.shape[0] + spare_rows, 2 * rows), jnp.float32)
+        whole = lax.dynamic_update_slice(whole, block, (0, 0))
+        return lax.dynamic_update_slice(whole, values, (block.shape[0], 0))
 
     raw_scores = []
     for k, span in enumerate((slice(0, cut), slice(cut, blocks))):
@@ -158,12 +158,12 @@
         lanes = keep.shape[0]
         part_scores = dot(send, text_raw, ((1,), (1,)))
         if k == 1:
-            part_scores = with_squares(part_scores, jnp.concatenate([squares[0], squares[2], squares[1]], axis=0))
+            part_scores = with_rows(part_scores, jnp.concatenate([squares[0], squares[2], squares[1]], axis=0))
         sent = swap(part_scores, core)
         mine = dot(keep, text_raw, ((1,), (1,))) + sent[:lanes]
         if k == 1:
             square_sum = jnp.concatenate(squares, axis=0) + sent[lanes : lanes + 1 + 2 * half_rows]
-            mine = with_squares(mine, square_sum)
+            mine = with_rows(mine, square_sum)
         mine = mine + swap(mine, far)
         raw_scores.append(mine[:lanes])
     inverse = lax.rsqrt(mine[lanes : lanes + 1 + 2 * half_rows] + EPSILON)
@@ -203,16 +203,17 @@
         - matches
     )
     weighted = grad * scores
-    along = jnp.concatenate([jnp.sum(weighted, axis=0), jnp.sum(weighted, axis=1)])
-    grad_other = swap(grad, core)
-    along_other = swap(along, core)
-    text_along = (along[: 2 * rows] + along_other[: 2 * rows])[:, None]
-    keep_along, send_along = along[2 * rows :, None], along_other[2 * rows :, None]
+    along = jnp.concatenate([as_rows(jnp.sum(weighted, axis=0)), as_rows(jnp.sum(weighted, axis=1))], axis=0)
+    moved = swap(with_rows(grad, along), core)
+    grad_other, along_other = moved[:half], moved[half : half + 1 + half_rows]
+    text_along = (along[0] + along_other[0])[:, None]
+    keep_along = along[1:].reshape(-1)[:half, None]
+    send_along = along_other[1:].reshape(-1)[:half, None]
 
     text_mine = lax.optimization_barrier(dot(grad, keep_unit, ((0,), (0,))))
     text_parts = []
-    for k in range(2):
-        cols = slice(k * (feat // 2), (k + 1) * (feat // 2))
+    for _ in range(1):
+        cols = slice(0, feat)
         cot = text_mine[:, cols] + dot(grad_other, send_unit[:, cols], ((0,), (0,)))
         text_parts.append((scale * cot - text_unit[:, cols] * text_along) * text_inverse)
     text_back = [one + swap(one, near) for one in text_parts]
@@ -235,7 +236,7 @@
         return jnp.concatenate([hidden_tile[:, q * slot : (q + 1) * slot] for q in which], axis=1)
 
     halves = []
-    for k in range(2):
+    for k in range(1):
         crossing = dot(hidden_of(outer), text_back[k], ((0,), (0,)))
         crossing = scatter_blocks([crossing[j * slot : (j + 1) * slot] for j in range(top)], moves[1:])
         halves.append(swap(crossing, moves[0]))

time: 75.9 us -> 79.1 us (1.042)
  waiting for transfers between devices: 28.7 us -> 33.7 us
  starting transfers between devices: 28.5 us -> 26.6 us
  local copies, waits for them, and re-layouts: 6.33 us -> 7.25 us
    ppermute x28 -> x24, waiting for transfers between devices: 28.7 us -> 33.7 us  [swap(): return lax.ppermute(block, axes if len(axes) > 1 else axes[0], route)]
    ppermute x28 -> x24, starting transfers between devices: 28.5 us -> 26.6 us  [swap(): return lax.ppermute(block, axes if len(axes) > 1 else axes[0], route)]
    dynamic_slice x4, local copies, waits for them, and re-layouts: 0.05 us -> 0.92 us  [body(): clip_send.append(lax.dynamic_slice_in_dim(one, (1 - own_core) * part, part))]
    dot_general x14 -> x12, matrix products: 6.36 us -> 5.77 us  [dot(): lax.dot_general(a, b, ((contract[0], contract[1]), ((), ())), precision=P...]
    dynamic_update_slice x4 -> x5, local copies, waits for them, and re-layouts: 2.11 us -> 2.13 us  [the longest x2 1.46 us: with_rows(): return lax.dynamic_update_slice(whole, values, (block.shape[0], 0))]
  transfers between devices with their start and end apart: 28 -> 24, of which waited for: 16 -> 13; matrix products, arithmetic and copies ran while one was open for 14% -> 13% of each run, Pallas kernels for 0% -> 0%
where the time goes in v1:
time: 79.1 us; the launch traced here: 78.8 us
  waiting for transfers between devices  33.7 us (43%)
  starting transfers between devices  26.6 us (34%)
  local copies, waits for them, and re-layouts  7.25 us (9%)
  matrix products  5.77 us (7%)
  other arithmetic  3.61 us (5%)
  between operations  1.92 us (2%)
    ppermute x24, waiting for transfers between devices, swap(): return lax.ppermute(block, axes if len(axes) > 1 else axes[0], route)  33.7 us
    ppermute x24, starting transfers between devices, swap(): return lax.ppermute(block, axes if len(axes) > 1 else axes[0], route)  26.6 us
    dot_general x12, matrix products, dot(): lax.dot_general(a, b, ((contract[0], contract[1]), ((), ())), precision=P...  5.77 us
    unnamed x23, local copies, waits for them, and re-layouts  3.49 us
  transfers between devices with their start and end apart: 24, of which 13 were waited for; matrix products, arithmetic and copies ran while one was open for 13% of the time, Pallas kernels for 0%

profile of v1, /device:TPU:0, one launch (start us, length us, event | category | flops | bytes accessed | tf_op | source)
XLA Modules:
  0.0 78.8 jit_solution(11996493593872894835)
XLA Ops:
  0.6 4.1 %collective-permute-start = (f32[128,256]{1,0:T(8,128)}, f32[128,256]{1,0:T(8,128)}, u32[]{:S(2)}, u32[]{:S(2)}) collective-permute-start(f32[128,256]{1,0:T(8,128)} %param.7), channel_id=1, source_target_pairs={{0,16},{8,24},{16,0},{24,8},{1,17},{9,25},{17,1},{25,9},{2,18},{10... | collective-permute-start | bytes 393224 | tf_op jit(solution)/shard_map/ppermute | solution.py:26
  4.8 1.5 %collective-permute-start.1 = (f32[128,256]{1,0:T(8,128)}, f32[128,256]{1,0:T(8,128)S(1)}, u32[]{:S(2)}, u32[]{:S(2)}) collective-permute-start(f32[128,256]{1,0:T(8,128)} %param.7), channel_id=1, source_target_pairs={{0,4},{4,0},{1,5},{5,1},{2,6},{6,2},{3,7},{7,3},{8,12},{12,8},{9,1... | collective-permute-start | bytes 393224 | tf_op jit(solution)/shard_map/ppermute | solution.py:26
  6.3 1.5 %constant_dynamic-update-slice_fusion.2 = (f32[256,256]{1,0:T(8,128)S(1)}, f32[128,256]{1,0:T(8,128)S(1)}) fusion(f32[256,256]{1,0:T(8,128)S(1)} %broadcast_in_dim.8, s32[]{:T(128)S(6)} %select_n.100, f32[128,1024]{1,0:T(8,128)} %param.5, f32[1024,256]{1,0:T(8,128)S(1)} %copy-done), kind=kOutput, calls=%fused_computation.88 | convolution fusion | flops 201326592 | bytes 1835012 | tf_op jit(solution)/shard_map/dot_general | solution.py:56
  7.8 1.6 %collective-permute-start.2 = (f32[128,256]{1,0:T(8,128)S(1)}, f32[128,256]{1,0:T(8,128)S(1)}, u32[]{:S(2)}, u32[]{:S(2)}) collective-permute-start(f32[128,256]{1,0:T(8,128)S(1)} %get-tuple-element.65), channel_id=1, source_target_pairs={{0,8},{8,0},{16,24},{24,16},{1,9},{9,1},{17,25},{25,17},{2,10},{10... | collective-permute-start | bytes 393224 | tf_op jit(solution)/shard_map/ppermute | solution.py:26
  9.5 0.7 copy-done.9
  10.7 0.5 collective-permute-start.12
  11.3 0.8 %copy-done.2 = f32[128,256]{1,0:T(8,128)S(1)} copy-done((f32[128,256]{1,0:T(8,128)S(1)}, f32[128,256]{1,0:T(8,128)}, u32[]{:S(2)}) %copy-start.2) | copy-done | bytes 131096
  12.9 0.9 %constant_dynamic-slice_fusion.13 = (f32[64,256]{1,0:T(8,128)S(1)}, f32[64,256]{1,0:T(8,128)S(1)}) fusion(f32[128,256]{1,0:T(8,128)} %collective-permute-done, s32[]{:T(128)S(6)} %select_n.102, s32[]{:T(128)S(6)} %select_n.98), kind=kLoop, calls=%fused_computation.85 | loop fusion | bytes 262152 | tf_op jit(solution)/shard_map/dynamic_slice | solution.py:102
  13.8 0.6 collective-permute-start.5
  15.0 4.1 %collective-permute-done.5 = f32[128,256]{1,0:T(8,128)S(1)} collective-permute-done((f32[128,256]{1,0:T(8,128)}, f32[128,256]{1,0:T(8,128)S(1)}, u32[]{:S(2)}, u32[]{:S(2)}) %collective-permute-start.5) | collective-permute-done | bytes 131104 | tf_op jit(solution)/shard_map/ppermute | solution.py:26
  19.3 0.6 dynamic_update_slice.32
  20.1 0.6 copy-done.5
  20.7 1.3 %dynamic_update_slice.33 = f32[72,256]{1,0:T(8,128)} dynamic-update-slice(f32[72,256]{1,0:T(8,128)} %dynamic_update_slice.32, f32[3,256]{1,0:T(4,128)S(1)} %fusion.43, s32[]{:T(128)} %constant.71.clone.1, s32[]{:T(128)} %constant.68.clone.1) | dynamic-update-slice | bytes 6148 | tf_op jit(solution)/shard_map/dynamic_update_slice | solution.py:152
  22.2 0.6 copy-done.10
  22.8 0.7 collective-permute-done.6
  23.9 0.6 copy-done.4
  24.7 1.6 %collective-permute-start.7 = (f32[72,256]{1,0:T(8,128)S(1)}, f32[72,256]{1,0:T(8,128)S(1)}, u32[]{:S(2)}, u32[]{:S(2)}) collective-permute-start(f32[72,256]{1,0:T(8,128)S(1)} %dynamic_update_slice.35), channel_id=1, source_target_pairs={{0,2},{1,3},{2,0},{3,1},{4,6},{5,7},{6,4},{7,5},{8,10},{9,11},{10,... | collective-permute-start | bytes 221192 | tf_op jit(solution)/shard_map/ppermute | solution.py:26
  26.6 0.6 collective-permute-start.4
  27.2 1.9 %collective-permute-done.7 = f32[72,256]{1,0:T(8,128)S(1)} collective-permute-done((f32[72,256]{1,0:T(8,128)S(1)}, f32[72,256]{1,0:T(8,128)S(1)}, u32[]{:S(2)}, u32[]{:S(2)}) %collective-permute-start.7) | collective-permute-done | bytes 73760 | tf_op jit(solution)/shard_map/ppermute | solution.py:26
  29.1 4.2 %collective-permute-done.4 = f32[192,256]{1,0:T(8,128)S(1)} collective-permute-done((f32[192,256]{1,0:T(8,128)S(1)}, f32[192,256]{1,0:T(8,128)S(1)}, u32[]{:S(2)}, u32[]{:S(2)}) %collective-permute-start.4) | collective-permute-done | bytes 196640 | tf_op jit(solution)/shard_map/ppermute | solution.py:26
  33.9 0.6 collective-permute-start.10
  34.5 3.0 %collective-permute-done.10 = f32[2,256]{1,0:T(2,128)S(1)} collective-permute-done((f32[2,256]{1,0:T(2,128)S(1)}, f32[2,256]{1,0:T(2,128)S(1)}, u32[]{:S(2)}, u32[]{:S(2)}) %collective-permute-start.10) | collective-permute-done | bytes 2080 | tf_op jit(solution)/shard_map/ppermute | solution.py:26
  37.6 0.4 collective-permute-start.11
  38.1 2.8 %collective-permute-start.9 = (f32[2,256]{1,0:T(2,128)S(1)}, f32[2,256]{1,0:T(2,128)S(1)}, u32[]{:S(2)}, u32[]{:S(2)}) collective-permute-start(f32[2,256]{1,0:T(2,128)S(1)} %pad_maximum_fusion.10), channel_id=1, source_target_pairs={{0,8},{8,0},{16,24},{24,16},{1,9},{9,1},{17,25},{25,17},{2,10},{10... | collective-permute-start | bytes 6152 | tf_op jit(solution)/shard_map/ppermute | solution.py:26
  40.9 1.3 %collective-permute-done.11 = f32[2,256]{1,0:T(2,128)S(1)} collective-permute-done((f32[2,256]{1,0:T(2,128)S(1)}, f32[2,256]{1,0:T(2,128)S(1)}, u32[]{:S(2)}, u32[]{:S(2)}) %collective-permute-start.11) | collective-permute-done | bytes 2080 | tf_op jit(solution)/shard_map/ppermute | solution.py:26
  43.3 1.1 %collective-permute-done.13 = f32[264,256]{1,0:T(8,128)S(1)} collective-permute-done((f32[264,256]{1,0:T(8,128)S(1)}, f32[264,256]{1,0:T(8,128)S(1)}, u32[]{:S(2)}, u32[]{:S(2)}) %collective-permute-start.13) | collective-permute-done | bytes 270368 | tf_op jit(solution)/shard_map/ppermute | solution.py:26
  44.8 1.6 %collective-permute-start.22 = (f32[128,256]{1,0:T(8,128)S(1)}, f32[128,256]{1,0:T(8,128)S(1)}, u32[]{:S(2)}, u32[]{:S(2)}) collective-permute-start(f32[128,256]{1,0:T(8,128)S(1)} %pad_maximum_fusion.4), channel_id=1, source_target_pairs={{0,4},{4,0},{1,5},{5,1},{2,6},{6,2},{3,7},{7,3},{8,12},{12,8},{9,1... | collective-permute-start | bytes 393224 | tf_op jit(solution)/shard_map/ppermute | solution.py:26
  46.4 0.4 fusion.17
  46.9 0.6 collective-permute-start.21
  47.5 3.8 %collective-permute-done.22 = f32[128,256]{1,0:T(8,128)S(1)} collective-permute-done((f32[128,256]{1,0:T(8,128)S(1)}, f32[128,256]{1,0:T(8,128)S(1)}, u32[]{:S(2)}, u32[]{:S(2)}) %collective-permute-start.22) | collective-permute-done | bytes 131104 | tf_op jit(solution)/shard_map/ppermute | solution.py:26
  51.3 1.9 %collective-permute-start.23 = (f32[128,256]{1,0:T(8,128)S(1)}, f32[128,256]{1,0:T(8,128)S(1)}, u32[]{:S(2)}, u32[]{:S(2)}) collective-permute-start(f32[128,256]{1,0:T(8,128)S(1)} %maximum_add_fusion.1), channel_id=1, source_target_pairs={{0,16},{8,24},{16,0},{24,8},{1,17},{9,25},{17,1},{25,9},{2,18},{10... | collective-permute-start | bytes 393224 | tf_op jit(solution)/shard_map/ppermute | solution.py:26
  53.2 0.5 fusion.3
  53.7 1.6 %collective-permute-start.14 = (f32[256,256]{1,0:T(8,128)S(1)}, f32[256,256]{1,0:T(8,128)S(1)}, u32[]{:S(2)}, u32[]{:S(2)}) collective-permute-start(f32[256,256]{1,0:T(8,128)S(1)} %fusion.3), channel_id=1, source_target_pairs={{0,8},{8,0},{16,24},{24,16},{1,9},{9,1},{17,25},{25,17},{2,10},{10... | collective-permute-start | bytes 786440 | tf_op jit(solution)/shard_map/ppermute | solution.py:26
  55.3 2.6 %collective-permute-done.23 = f32[128,256]{1,0:T(8,128)S(1)} collective-permute-done((f32[128,256]{1,0:T(8,128)S(1)}, f32[128,256]{1,0:T(8,128)S(1)}, u32[]{:S(2)}, u32[]{:S(2)}) %collective-permute-start.23) | collective-permute-done | bytes 131104 | tf_op jit(solution)/shard_map/ppermute | solution.py:26
  58.0 0.7 maximum_select_fusion
  58.7 3.1 %collective-permute-done.14 = f32[256,256]{1,0:T(8,128)S(1)} collective-permute-done((f32[256,256]{1,0:T(8,128)S(1)}, f32[256,256]{1,0:T(8,128)S(1)}, u32[]{:S(2)}, u32[]{:S(2)}) %collective-permute-start.14) | collective-permute-done | bytes 262176 | tf_op jit(solution)/shard_map/ppermute | solution.py:26
  61.8 0.7 fusion.36
  62.5 0.5 collective-permute-start.16
  63.0 0.4 fusion.10
  63.5 1.6 %collective-permute-start.19 = (f32[128,256]{1,0:T(8,128)S(1)}, f32[128,256]{1,0:T(8,128)S(1)}, u32[]{:S(2)}, u32[]{:S(2)}) collective-permute-start(f32[128,256]{1,0:T(8,128)S(1)} %slice.223), channel_id=1, source_target_pairs={{0,4},{4,0},{1,5},{5,1},{2,6},{6,2},{3,7},{7,3},{8,12},{12,8},{9,1... | collective-permute-start | bytes 393224 | tf_op jit(solution)/shard_map/ppermute | solution.py:26
  65.0 0.4 fusion.6
  65.4 0.6 collective-permute-start.18
  66.0 3.9 %collective-permute-done.19 = f32[128,256]{1,0:T(8,128)S(1)} collective-permute-done((f32[128,256]{1,0:T(8,128)S(1)}, f32[128,256]{1,0:T(8,128)S(1)}, u32[]{:S(2)}, u32[]{:S(2)}) %collective-permute-start.19) | collective-permute-done | bytes 131104 | tf_op jit(solution)/shard_map/ppermute | solution.py:26
  69.9 2.1 %collective-permute-start.20 = (f32[128,256]{1,0:T(8,128)S(1)}, f32[128,256]{1,0:T(8,128)S(1)}, u32[]{:S(2)}, u32[]{:S(2)}) collective-permute-start(f32[128,256]{1,0:T(8,128)S(1)} %slice_add_fusion), channel_id=1, source_target_pairs={{0,16},{8,24},{16,0},{24,8},{1,17},{9,25},{17,1},{25,9},{2,18},{10... | collective-permute-start | bytes 393224 | tf_op jit(solution)/shard_map/ppermute | solution.py:26
  72.0 1.5 %collective-permute-start.17 = (f32[128,256]{1,0:T(8,128)S(1)}, f32[128,256]{1,0:T(8,128)S(1)}, u32[]{:S(2)}, u32[]{:S(2)}) collective-permute-start(f32[128,256]{1,0:T(8,128)S(1)} %dynamic-slice_add_fusion), channel_id=1, source_target_pairs={{0,2},{1,3},{2,0},{3,1},{4,6},{5,7},{6,4},{7,5},{8,10},{9,11},{10,... | collective-permute-start | bytes 393224 | tf_op jit(solution)/shard_map/ppermute | solution.py:26
  73.6 3.9 %collective-permute-done.20 = f32[128,256]{1,0:T(8,128)S(1)} collective-permute-done((f32[128,256]{1,0:T(8,128)S(1)}, f32[128,256]{1,0:T(8,128)S(1)}, u32[]{:S(2)}, u32[]{:S(2)}) %collective-permute-start.20) | collective-permute-done | bytes 131104 | tf_op jit(solution)/shard_map/ppermute | solution.py:26
  77.4 0.7 fusion.34
  78.1 0.7 add_add_fusion
  (100 shorter events, 4.9 us)
Async XLA Ops:
  0.6 5.7 %copy-start = (f32[1024,256]{1,0:T(8,128)S(1)}, f32[1024,256]{1,0:T(8,128)}, u32[]{:S(2)}) copy-start(f32[1024,256]{1,0:T(8,128)} %param.6) | copy-start | bytes 3145732
  0.6 12.2 %collective-permute-start = (f32[128,256]{1,0:T(8,128)}, f32[128,256]{1,0:T(8,128)}, u32[]{:S(2)}, u32[]{:S(2)}) collective-permute-start(f32[128,256]{1,0:T(8,128)} %param.7), channel_id=1, source_target_pairs={{0,16},{8,24},{16,0},{24,8},{1,17},{9,25},{17,1},{25,9},{2,18},{10... | collective-permute-start | bytes 393224 | tf_op jit(solution)/shard_map/ppermute | solution.py:26
  4.8 9.6 %collective-permute-start.1 = (f32[128,256]{1,0:T(8,128)}, f32[128,256]{1,0:T(8,128)S(1)}, u32[]{:S(2)}, u32[]{:S(2)}) collective-permute-start(f32[128,256]{1,0:T(8,128)} %param.7), channel_id=1, source_target_pairs={{0,4},{4,0},{1,5},{5,1},{2,6},{6,2},{3,7},{7,3},{8,12},{12,8},{9,1... | collective-permute-start | bytes 393224 | tf_op jit(solution)/shard_map/ppermute | solution.py:26
  6.3 3.8 %copy-start.1 = (f32[128,1024]{1,0:T(8,128)S(1)}, f32[128,1024]{1,0:T(8,128)}, u32[]{:S(2)}) copy-start(f32[128,1024]{1,0:T(8,128)} %param.5) | copy-start | bytes 1572868
  7.8 6.6 %collective-permute-start.2 = (f32[128,256]{1,0:T(8,128)S(1)}, f32[128,256]{1,0:T(8,128)S(1)}, u32[]{:S(2)}, u32[]{:S(2)}) collective-permute-start(f32[128,256]{1,0:T(8,128)S(1)} %get-tuple-element.65), channel_id=1, source_target_pairs={{0,8},{8,0},{16,24},{24,16},{1,9},{9,1},{17,25},{25,17},{2,10},{10... | collective-permute-start | bytes 393224 | tf_op jit(solution)/shard_map/ppermute | solution.py:26
  9.5 0.7 copy-start.9
  10.7 11.4 %collective-permute-start.12 = (f32[129,512]{1,0:T(8,128)S(1)}, f32[129,512]{1,0:T(8,128)S(1)}, u32[]{:S(2)}, u32[]{:S(2)}) collective-permute-start(f32[129,512]{1,0:T(8,128)S(1)} %pad_maximum_fusion), channel_id=1, source_target_pairs={{0,8},{8,0},{16,24},{24,16},{1,9},{9,1},{17,25},{25,17},{2,10},{10... | collective-permute-start | bytes 792584 | tf_op jit(solution)/shard_map/ppermute | solution.py:26
  11.3 0.9 %copy-start.2 = (f32[128,256]{1,0:T(8,128)S(1)}, f32[128,256]{1,0:T(8,128)}, u32[]{:S(2)}) copy-start(f32[128,256]{1,0:T(8,128)} %param.7) | copy-start | bytes 393220
  13.8 5.2 %collective-permute-start.5 = (f32[128,256]{1,0:T(8,128)}, f32[128,256]{1,0:T(8,128)S(1)}, u32[]{:S(2)}, u32[]{:S(2)}) collective-permute-start(f32[128,256]{1,0:T(8,128)} %collective-permute-done), channel_id=1, source_target_pairs={{0,4},{4,0},{1,5},{5,1},{2,6},{6,2},{3,7},{7,3},{8,12},{12,8},{9,1... | collective-permute-start | bytes 393224 | tf_op jit(solution)/shard_map/ppermute | solution.py:26
  14.8 11.5 %collective-permute-start.3 = (f32[192,256]{1,0:T(8,128)S(1)}, f32[192,256]{1,0:T(8,128)S(1)}, u32[]{:S(2)}, u32[]{:S(2)}) collective-permute-start(f32[192,256]{1,0:T(8,128)S(1)} %fusion.28), channel_id=1, source_target_pairs={{0,1},{1,0},{2,3},{3,2},{4,5},{5,4},{6,7},{7,6},{8,9},{9,8},{10,11... | collective-permute-start | bytes 589832 | tf_op jit(solution)/shard_map/ppermute | solution.py:26
  15.0 5.2 %copy-start.3 = (f32[256]{0:T(256)}, f32[256]{0:T(256)S(1)}, u32[]{:S(2)}) copy-start(f32[256]{0:T(256)S(1)} %multiply_reduce_fusion.2) | copy-start | bytes 3076
  20.1 0.6 copy-start.5
  20.1 0.6 copy-start.7
  22.0 1.5 %collective-permute-start.6 = (f32[72,256]{1,0:T(8,128)}, f32[72,256]{1,0:T(8,128)S(1)}, u32[]{:S(2)}, u32[]{:S(2)}) collective-permute-start(f32[72,256]{1,0:T(8,128)} %dynamic_update_slice.33), channel_id=1, source_target_pairs={{0,1},{1,0},{2,3},{3,2},{4,5},{5,4},{6,7},{7,6},{8,9},{9,8},{10,11... | collective-permute-start | bytes 221192 | tf_op jit(solution)/shard_map/ppermute | solution.py:26
  22.1 0.7 copy-start.10
  23.8 0.7 copy-start.4
  23.8 0.7 copy-start.6
  23.8 0.7 copy-start.8
  24.7 4.4 %collective-permute-start.7 = (f32[72,256]{1,0:T(8,128)S(1)}, f32[72,256]{1,0:T(8,128)S(1)}, u32[]{:S(2)}, u32[]{:S(2)}) collective-permute-start(f32[72,256]{1,0:T(8,128)S(1)} %dynamic_update_slice.35), channel_id=1, source_target_pairs={{0,2},{1,3},{2,0},{3,1},{4,6},{5,7},{6,4},{7,5},{8,10},{9,11},{10,... | collective-permute-start | bytes 221192 | tf_op jit(solution)/shard_map/ppermute | solution.py:26
  26.6 6.7 %collective-permute-start.4 = (f32[192,256]{1,0:T(8,128)S(1)}, f32[192,256]{1,0:T(8,128)S(1)}, u32[]{:S(2)}, u32[]{:S(2)}) collective-permute-start(f32[192,256]{1,0:T(8,128)S(1)} %convolution_add_fusion.1), channel_id=1, source_target_pairs={{0,2},{1,3},{2,0},{3,1},{4,6},{5,7},{6,4},{7,5},{8,10},{9,11},{10,... | collective-permute-start | bytes 589832 | tf_op jit(solution)/shard_map/ppermute | solution.py:26
  33.9 3.7 %collective-permute-start.10 = (f32[2,256]{1,0:T(2,128)S(1)}, f32[2,256]{1,0:T(2,128)S(1)}, u32[]{:S(2)}, u32[]{:S(2)}) collective-permute-start(f32[2,256]{1,0:T(2,128)S(1)} %pad_maximum_fusion.11), channel_id=1, source_target_pairs={{0,4},{4,0},{1,5},{5,1},{2,6},{6,2},{3,7},{7,3},{8,12},{12,8},{9,1... | collective-permute-start | bytes 6152 | tf_op jit(solution)/shard_map/ppermute | solution.py:26
  34.5 3.5 %collective-permute-start.8 = (f32[2,256]{1,0:T(2,128)S(1)}, f32[2,256]{1,0:T(2,128)S(1)}, u32[]{:S(2)}, u32[]{:S(2)}) collective-permute-start(f32[2,256]{1,0:T(2,128)S(1)} %pad_maximum_fusion.9), channel_id=1, source_target_pairs={{0,1},{1,0},{2,3},{3,2},{4,5},{5,4},{6,7},{7,6},{8,9},{9,8},{10,11... | collective-permute-start | bytes 6152 | tf_op jit(solution)/shard_map/ppermute | solution.py:26
  37.6 4.5 %collective-permute-start.11 = (f32[2,256]{1,0:T(2,128)S(1)}, f32[2,256]{1,0:T(2,128)S(1)}, u32[]{:S(2)}, u32[]{:S(2)}) collective-permute-start(f32[2,256]{1,0:T(2,128)S(1)} %pad_maximum_fusion.12), channel_id=1, source_target_pairs={{0,16},{8,24},{16,0},{24,8},{1,17},{9,25},{17,1},{25,9},{2,18},{10... | collective-permute-start | bytes 6152 | tf_op jit(solution)/shard_map/ppermute | solution.py:26
  38.1 4.4 %collective-permute-start.9 = (f32[2,256]{1,0:T(2,128)S(1)}, f32[2,256]{1,0:T(2,128)S(1)}, u32[]{:S(2)}, u32[]{:S(2)}) collective-permute-start(f32[2,256]{1,0:T(2,128)S(1)} %pad_maximum_fusion.10), channel_id=1, source_target_pairs={{0,8},{8,0},{16,24},{24,16},{1,9},{9,1},{17,25},{25,17},{2,10},{10... | collective-permute-start | bytes 6152 | tf_op jit(solution)/shard_map/ppermute | solution.py:26
  42.8 1.6 %collective-permute-start.13 = (f32[264,256]{1,0:T(8,128)S(1)}, f32[264,256]{1,0:T(8,128)S(1)}, u32[]{:S(2)}, u32[]{:S(2)}) collective-permute-start(f32[264,256]{1,0:T(8,128)S(1)} %constant_dynamic-update-slice_fusion), channel_id=1, source_target_pairs={{0,1},{1,0},{2,3},{3,2},{4,5},{5,4},{6,7},{7,6},{8,9},{9,8},{10,11... | collective-permute-start | bytes 811016 | tf_op jit(solution)/shard_map/ppermute | solution.py:26
  44.8 6.4 %collective-permute-start.22 = (f32[128,256]{1,0:T(8,128)S(1)}, f32[128,256]{1,0:T(8,128)S(1)}, u32[]{:S(2)}, u32[]{:S(2)}) collective-permute-start(f32[128,256]{1,0:T(8,128)S(1)} %pad_maximum_fusion.4), channel_id=1, source_target_pairs={{0,4},{4,0},{1,5},{5,1},{2,6},{6,2},{3,7},{7,3},{8,12},{12,8},{9,1... | collective-permute-start | bytes 393224 | tf_op jit(solution)/shard_map/ppermute | solution.py:26
  46.9 8.4 %collective-permute-start.21 = (f32[128,256]{1,0:T(8,128)S(1)}, f32[128,256]{1,0:T(8,128)S(1)}, u32[]{:S(2)}, u32[]{:S(2)}) collective-permute-start(f32[128,256]{1,0:T(8,128)S(1)} %pad_maximum_fusion.3), channel_id=1, source_target_pairs={{0,4},{4,0},{1,5},{5,1},{2,6},{6,2},{3,7},{7,3},{8,12},{12,8},{9,1... | collective-permute-start | bytes 393224 | tf_op jit(solution)/shard_map/ppermute | solution.py:26
  51.3 6.6 %collective-permute-start.23 = (f32[128,256]{1,0:T(8,128)S(1)}, f32[128,256]{1,0:T(8,128)S(1)}, u32[]{:S(2)}, u32[]{:S(2)}) collective-permute-start(f32[128,256]{1,0:T(8,128)S(1)} %maximum_add_fusion.1), channel_id=1, source_target_pairs={{0,16},{8,24},{16,0},{24,8},{1,17},{9,25},{17,1},{25,9},{2,18},{10... | collective-permute-start | bytes 393224 | tf_op jit(solution)/shard_map/ppermute | solution.py:26
  53.7 8.1 %collective-permute-start.14 = (f32[256,256]{1,0:T(8,128)S(1)}, f32[256,256]{1,0:T(8,128)S(1)}, u32[]{:S(2)}, u32[]{:S(2)}) collective-permute-start(f32[256,256]{1,0:T(8,128)S(1)} %fusion.3), channel_id=1, source_target_pairs={{0,8},{8,0},{16,24},{24,16},{1,9},{9,1},{17,25},{25,17},{2,10},{10... | collective-permute-start | bytes 786440 | tf_op jit(solution)/shard_map/ppermute | solution.py:26
  62.5 15.6 %collective-permute-start.15 = (f32[128,256]{1,0:T(8,128)S(1)}, f32[128,256]{1,0:T(8,128)S(1)}, u32[]{:S(2)}, u32[]{:S(2)}) collective-permute-start(f32[128,256]{1,0:T(8,128)S(1)} %get-tuple-element.28), channel_id=1, source_target_pairs={{0,1},{1,0},{2,3},{3,2},{4,5},{5,4},{6,7},{7,6},{8,9},{9,8},{10,11... | collective-permute-start | bytes 393224 | tf_op jit(solution)/shard_map/ppermute | solution.py:26
  62.5 9.5 %collective-permute-start.16 = (f32[128,256]{1,0:T(8,128)S(1)}, f32[128,256]{1,0:T(8,128)S(1)}, u32[]{:S(2)}, u32[]{:S(2)}) collective-permute-start(f32[128,256]{1,0:T(8,128)S(1)} %get-tuple-element.29), channel_id=1, source_target_pairs={{0,1},{1,0},{2,3},{3,2},{4,5},{5,4},{6,7},{7,6},{8,9},{9,8},{10,11... | collective-permute-start | bytes 393224 | tf_op jit(solution)/shard_map/ppermute | solution.py:26
  63.5 6.4 %collective-permute-start.19 = (f32[128,256]{1,0:T(8,128)S(1)}, f32[128,256]{1,0:T(8,128)S(1)}, u32[]{:S(2)}, u32[]{:S(2)}) collective-permute-start(f32[128,256]{1,0:T(8,128)S(1)} %slice.223), channel_id=1, source_target_pairs={{0,4},{4,0},{1,5},{5,1},{2,6},{6,2},{3,7},{7,3},{8,12},{12,8},{9,1... | collective-permute-start | bytes 393224 | tf_op jit(solution)/shard_map/ppermute | solution.py:26
  65.4 8.1 %collective-permute-start.18 = (f32[128,256]{1,0:T(8,128)S(1)}, f32[128,256]{1,0:T(8,128)S(1)}, u32[]{:S(2)}, u32[]{:S(2)}) collective-permute-start(f32[128,256]{1,0:T(8,128)S(1)} %slice.219), channel_id=1, source_target_pairs={{0,4},{4,0},{1,5},{5,1},{2,6},{6,2},{3,7},{7,3},{8,12},{12,8},{9,1... | collective-permute-start | bytes 393224 | tf_op jit(solution)/shard_map/ppermute | solution.py:26
  69.9 7.5 %collective-permute-start.20 = (f32[128,256]{1,0:T(8,128)S(1)}, f32[128,256]{1,0:T(8,128)S(1)}, u32[]{:S(2)}, u32[]{:S(2)}) collective-permute-start(f32[128,256]{1,0:T(8,128)S(1)} %slice_add_fusion), channel_id=1, source_target_pairs={{0,16},{8,24},{16,0},{24,8},{1,17},{9,25},{17,1},{25,9},{2,18},{10... | collective-permute-start | bytes 393224 | tf_op jit(solution)/shard_map/ppermute | solution.py:26
  72.0 6.1 %collective-permute-start.17 = (f32[128,256]{1,0:T(8,128)S(1)}, f32[128,256]{1,0:T(8,128)S(1)}, u32[]{:S(2)}, u32[]{:S(2)}) collective-permute-start(f32[128,256]{1,0:T(8,128)S(1)} %dynamic-slice_add_fusion), channel_id=1, source_target_pairs={{0,2},{1,3},{2,0},{3,1},{4,6},{5,7},{6,4},{7,5},{8,10},{9,11},{10,... | collective-permute-start | bytes 393224 | tf_op jit(solution)/shard_map/ppermute | solution.py:26

commit v2 on v1

--- a/solution.py
+++ b/solution.py
@@ -212,8 +212,8 @@
 
     text_mine = lax.optimization_barrier(dot(grad, keep_unit, ((0,), (0,))))
     text_parts = []
-    for _ in range(1):
-        cols = slice(0, feat)
+    for k in range(2):
+        cols = slice(k * (feat // 2), (k + 1) * (feat // 2))
         cot = text_mine[:, cols] + dot(grad_other, send_unit[:, cols], ((0,), (0,)))
         text_parts.append((scale * cot - text_unit[:, cols] * text_along) * text_inverse)
     text_back = [one + swap(one, near) for one in text_parts]
@@ -236,7 +236,7 @@
         return jnp.concatenate([hidden_tile[:, q * slot : (q + 1) * slot] for q in which], axis=1)
 
     halves = []
-    for k in range(1):
+    for k in range(2):
         crossing = dot(hidden_of(outer), text_back[k], ((0,), (0,)))
         crossing = scatter_blocks([crossing[j * slot : (j + 1) * slot] for j in range(top)], moves[1:])
         halves.append(swap(crossing, moves[0]))

time: 79.1 us -> 75.5 us (0.954)
  waiting for transfers between devices: 33.7 us -> 28.8 us
  starting transfers between devices: 26.6 us -> 28 us
  local copies, waits for them, and re-layouts: 7.25 us -> 6.34 us
    ppermute x24 -> x27, waiting for transfers between devices: 33.7 us -> 28.8 us  [swap(): return lax.ppermute(block, axes if len(axes) > 1 else axes[0], route)]
    ppermute x24 -> x27, starting transfers between devices: 26.6 us -> 28 us  [swap(): return lax.ppermute(block, axes if len(axes) > 1 else axes[0], route)]
    dynamic_slice x4, local copies, waits for them, and re-layouts: 0.92 us -> 0.05 us  [body(): clip_send.append(lax.dynamic_slice_in_dim(one, (1 - own_core) * part, part))]
    dot_general x12 -> x14, matrix products: 5.77 us -> 6.36 us  [dot(): lax.dot_general(a, b, ((contract[0], contract[1]), ((), ())), precision=P...]
  transfers between devices with their start and end apart: 24 -> 27, of which waited for: 13 -> 16; matrix products, arithmetic and copies ran while one was open for 13% -> 14% of each run, Pallas kernels for 0% -> 0%
where the time goes in v2:
time: 75.5 us; the launch traced here: 75.3 us
  waiting for transfers between devices  28.8 us (38%)
  starting transfers between devices  28 us (37%)
  matrix products  6.36 us (8%)
  local copies, waits for them, and re-layouts  6.34 us (8%)
  other arithmetic  3.81 us (5%)
  between operations  1.94 us (3%)
    ppermute x27, waiting for transfers between devices, swap(): return lax.ppermute(block, axes if len(axes) > 1 else axes[0], route)  28.8 us
    ppermute x27, starting transfers between devices, swap(): return lax.ppermute(block, axes if len(axes) > 1 else axes[0], route)  28 us
    dot_general x14, matrix products, dot(): lax.dot_general(a, b, ((contract[0], contract[1]), ((), ())), precision=P...  6.36 us
    unnamed x23, local copies, waits for them, and re-layouts  3.47 us
  transfers between devices with their start and end apart: 27, of which 16 were waited for; matrix products, arithmetic and copies ran while one was open for 14% of the time, Pallas kernels for 0%

profile of v2, /device:TPU:0, one launch (start us, length us, event | category | flops | bytes accessed | tf_op | source)
XLA Modules:
  0.0 75.3 jit_solution(3905683187082614306)
XLA Ops:
  0.6 4.1 %collective-permute-start = (f32[128,256]{1,0:T(8,128)}, f32[128,256]{1,0:T(8,128)S(1)}, u32[]{:S(2)}, u32[]{:S(2)}) collective-permute-start(f32[128,256]{1,0:T(8,128)} %param.7), channel_id=1, source_target_pairs={{0,16},{8,24},{16,0},{24,8},{1,17},{9,25},{17,1},{25,9},{2,18},{10... | collective-permute-start | bytes 393224 | tf_op jit(solution)/shard_map/ppermute | solution.py:26
  4.8 1.5 %collective-permute-start.1 = (f32[128,256]{1,0:T(8,128)}, f32[128,256]{1,0:T(8,128)S(1)}, u32[]{:S(2)}, u32[]{:S(2)}) collective-permute-start(f32[128,256]{1,0:T(8,128)} %param.7), channel_id=1, source_target_pairs={{0,4},{4,0},{1,5},{5,1},{2,6},{6,2},{3,7},{7,3},{8,12},{12,8},{9,1... | collective-permute-start | bytes 393224 | tf_op jit(solution)/shard_map/ppermute | solution.py:26
  6.3 1.5 %constant_dynamic-update-slice_fusion.2 = (f32[256,256]{1,0:T(8,128)S(1)}, f32[128,256]{1,0:T(8,128)S(1)}) fusion(f32[256,256]{1,0:T(8,128)S(1)} %broadcast_in_dim.8, s32[]{:T(128)S(6)} %select_n.100, f32[128,1024]{1,0:T(8,128)} %param.5, f32[1024,256]{1,0:T(8,128)S(1)} %copy-done), kind=kOutput, calls=%fused_computation.96 | convolution fusion | flops 201326592 | bytes 1835012 | tf_op jit(solution)/shard_map/dot_general | solution.py:56
  7.8 1.6 %collective-permute-start.2 = (f32[128,256]{1,0:T(8,128)S(1)}, f32[128,256]{1,0:T(8,128)S(1)}, u32[]{:S(2)}, u32[]{:S(2)}) collective-permute-start(f32[128,256]{1,0:T(8,128)S(1)} %get-tuple-element.65), channel_id=1, source_target_pairs={{0,8},{8,0},{16,24},{24,16},{1,9},{9,1},{17,25},{25,17},{2,10},{10... | collective-permute-start | bytes 393224 | tf_op jit(solution)/shard_map/ppermute | solution.py:26
  9.5 0.7 copy-done.9
  10.7 0.5 collective-permute-start.12
  11.3 0.8 %copy-done.2 = f32[128,256]{1,0:T(8,128)S(1)} copy-done((f32[128,256]{1,0:T(8,128)S(1)}, f32[128,256]{1,0:T(8,128)}, u32[]{:S(2)}) %copy-start.2) | copy-done | bytes 131096
  12.9 0.6 collective-permute-start.5
  13.5 0.7 collective-permute-done.2
  14.8 3.1 %collective-permute-done.5 = f32[128,256]{1,0:T(8,128)S(1)} collective-permute-done((f32[128,256]{1,0:T(8,128)S(1)}, f32[128,256]{1,0:T(8,128)S(1)}, u32[]{:S(2)}, u32[]{:S(2)}) %collective-permute-start.5) | collective-permute-done | bytes 131104 | tf_op jit(solution)/shard_map/ppermute | solution.py:26
  18.2 0.6 dynamic_update_slice.32
  19.1 0.5 copy-done.5
  19.6 1.3 %dynamic_update_slice.33 = f32[72,256]{1,0:T(8,128)} dynamic-update-slice(f32[72,256]{1,0:T(8,128)} %dynamic_update_slice.32, f32[3,256]{1,0:T(4,128)S(1)} %fusion.41, s32[]{:T(128)} %constant.71.clone.1, s32[]{:T(128)} %constant.68.clone.1) | dynamic-update-slice | bytes 6148 | tf_op jit(solution)/shard_map/dynamic_update_slice | solution.py:152
  21.0 0.6 copy-done.10
  21.7 0.7 collective-permute-done.6
  22.7 0.6 copy-done.4
  23.6 1.6 %collective-permute-start.7 = (f32[72,256]{1,0:T(8,128)S(1)}, f32[72,256]{1,0:T(8,128)S(1)}, u32[]{:S(2)}, u32[]{:S(2)}) collective-permute-start(f32[72,256]{1,0:T(8,128)S(1)} %dynamic_update_slice.35), channel_id=1, source_target_pairs={{0,2},{1,3},{2,0},{3,1},{4,6},{5,7},{6,4},{7,5},{8,10},{9,11},{10,... | collective-permute-start | bytes 221192 | tf_op jit(solution)/shard_map/ppermute | solution.py:26
  25.5 0.6 collective-permute-start.4
  26.1 1.9 %collective-permute-done.7 = f32[72,256]{1,0:T(8,128)S(1)} collective-permute-done((f32[72,256]{1,0:T(8,128)S(1)}, f32[72,256]{1,0:T(8,128)S(1)}, u32[]{:S(2)}, u32[]{:S(2)}) %collective-permute-start.7) | collective-permute-done | bytes 73760 | tf_op jit(solution)/shard_map/ppermute | solution.py:26
  28.2 4.0 %collective-permute-done.4 = f32[192,256]{1,0:T(8,128)S(1)} collective-permute-done((f32[192,256]{1,0:T(8,128)S(1)}, f32[192,256]{1,0:T(8,128)S(1)}, u32[]{:S(2)}, u32[]{:S(2)}) %collective-permute-start.4) | collective-permute-done | bytes 196640 | tf_op jit(solution)/shard_map/ppermute | solution.py:26
  32.8 0.6 collective-permute-start.10
  33.4 3.0 %collective-permute-done.10 = f32[2,256]{1,0:T(2,128)S(1)} collective-permute-done((f32[2,256]{1,0:T(2,128)S(1)}, f32[2,256]{1,0:T(2,128)S(1)}, u32[]{:S(2)}, u32[]{:S(2)}) %collective-permute-start.10) | collective-permute-done | bytes 2080 | tf_op jit(solution)/shard_map/ppermute | solution.py:26
  36.9 2.7 %collective-permute-start.9 = (f32[2,256]{1,0:T(2,128)S(1)}, f32[2,256]{1,0:T(2,128)S(1)}, u32[]{:S(2)}, u32[]{:S(2)}) collective-permute-start(f32[2,256]{1,0:T(2,128)S(1)} %pad_maximum_fusion.14), channel_id=1, source_target_pairs={{0,8},{8,0},{16,24},{24,16},{1,9},{9,1},{17,25},{25,17},{2,10},{10... | collective-permute-start | bytes 6152 | tf_op jit(solution)/shard_map/ppermute | solution.py:26
  39.7 1.4 %collective-permute-done.11 = f32[2,256]{1,0:T(2,128)S(1)} collective-permute-done((f32[2,256]{1,0:T(2,128)S(1)}, f32[2,256]{1,0:T(2,128)S(1)}, u32[]{:S(2)}, u32[]{:S(2)}) %collective-permute-start.11) | collective-permute-done | bytes 2080 | tf_op jit(solution)/shard_map/ppermute | solution.py:26
  42.0 0.4 fusion.13
  42.5 0.8 %collective-permute-done.13 = f32[264,256]{1,0:T(8,128)S(1)} collective-permute-done((f32[264,256]{1,0:T(8,128)S(1)}, f32[264,256]{1,0:T(8,128)S(1)}, u32[]{:S(2)}, u32[]{:S(2)}) %collective-permute-start.13) | collective-permute-done | bytes 270368 | tf_op jit(solution)/shard_map/ppermute | solution.py:26
  43.6 0.4 fusion.7
  44.0 2.1 %collective-permute-start.14 = (f32[256,128]{1,0:T(8,128)S(1)}, f32[256,128]{1,0:T(8,128)S(1)}, u32[]{:S(2)}, u32[]{:S(2)}) collective-permute-start(f32[256,128]{1,0:T(8,128)S(1)} %fusion.7), channel_id=1, source_target_pairs={{0,8},{8,0},{16,24},{24,16},{1,9},{9,1},{17,25},{25,17},{2,10},{10... | collective-permute-start | bytes 393224 | tf_op jit(solution)/shard_map/ppermute | solution.py:26
  46.5 1.6 %collective-permute-start.24 = (f32[128,256]{1,0:T(8,128)S(1)}, f32[128,256]{1,0:T(8,128)S(1)}, u32[]{:S(2)}, u32[]{:S(2)}) collective-permute-start(f32[128,256]{1,0:T(8,128)S(1)} %pad_maximum_fusion.8), channel_id=1, source_target_pairs={{0,4},{4,0},{1,5},{5,1},{2,6},{6,2},{3,7},{7,3},{8,12},{12,8},{9,1... | collective-permute-start | bytes 393224 | tf_op jit(solution)/shard_map/ppermute | solution.py:26
  48.1 0.6 collective-permute-start.25
  48.7 1.7 %collective-permute-done.14 = f32[256,128]{1,0:T(8,128)S(1)} collective-permute-done((f32[256,128]{1,0:T(8,128)S(1)}, f32[256,128]{1,0:T(8,128)S(1)}, u32[]{:S(2)}, u32[]{:S(2)}) %collective-permute-start.14) | collective-permute-done | bytes 131104 | tf_op jit(solution)/shard_map/ppermute | solution.py:26
  50.4 2.2 %collective-permute-done.15 = f32[256,128]{1,0:T(8,128)S(1)} collective-permute-done((f32[256,128]{1,0:T(8,128)S(1)}, f32[256,128]{1,0:T(8,128)S(1)}, u32[]{:S(2)}, u32[]{:S(2)}) %collective-permute-start.15) | collective-permute-done | bytes 131104 | tf_op jit(solution)/shard_map/ppermute | solution.py:26
  52.7 0.7 fusion.33
  54.1 0.6 collective-permute-done.25
  54.7 1.7 %collective-permute-start.26 = (f32[128,256]{1,0:T(8,128)S(1)}, f32[128,256]{1,0:T(8,128)S(1)}, u32[]{:S(2)}, u32[]{:S(2)}) collective-permute-start(f32[128,256]{1,0:T(8,128)S(1)} %maximum_add_fusion.1), channel_id=1, source_target_pairs={{0,16},{8,24},{16,0},{24,8},{1,17},{9,25},{17,1},{25,9},{2,18},{10... | collective-permute-start | bytes 393224 | tf_op jit(solution)/shard_map/ppermute | solution.py:26
  56.5 0.5 collective-permute-start.17
  57.0 0.9 %collective-permute-start.20 = (f32[128,128]{1,0:T(8,128)S(1)}, f32[128,128]{1,0:T(8,128)S(1)}, u32[]{:S(2)}, u32[]{:S(2)}) collective-permute-start(f32[128,128]{1,0:T(8,128)S(1)} %slice.263), channel_id=1, source_target_pairs={{0,4},{4,0},{1,5},{5,1},{2,6},{6,2},{3,7},{7,3},{8,12},{12,8},{9,1... | collective-permute-start | bytes 196616 | tf_op jit(solution)/shard_map/ppermute | solution.py:26
  58.3 3.0 %collective-permute-done.20 = f32[128,128]{1,0:T(8,128)S(1)} collective-permute-done((f32[128,128]{1,0:T(8,128)S(1)}, f32[128,128]{1,0:T(8,128)S(1)}, u32[]{:S(2)}, u32[]{:S(2)}) %collective-permute-start.20) | collective-permute-done | bytes 65568 | tf_op jit(solution)/shard_map/ppermute | solution.py:26
  61.4 0.8 %collective-permute-start.22 = (f32[128,128]{1,0:T(8,128)S(1)}, f32[128,128]{1,0:T(8,128)S(1)}, u32[]{:S(2)}, u32[]{:S(2)}) collective-permute-start(f32[128,128]{1,0:T(8,128)S(1)} %slice.265), channel_id=1, source_target_pairs={{0,4},{4,0},{1,5},{5,1},{2,6},{6,2},{3,7},{7,3},{8,12},{12,8},{9,1... | collective-permute-start | bytes 196616 | tf_op jit(solution)/shard_map/ppermute | solution.py:26
  62.2 3.4 %collective-permute-done.22 = f32[128,128]{1,0:T(8,128)S(1)} collective-permute-done((f32[128,128]{1,0:T(8,128)S(1)}, f32[128,128]{1,0:T(8,128)S(1)}, u32[]{:S(2)}, u32[]{:S(2)}) %collective-permute-start.22) | collective-permute-done | bytes 65568 | tf_op jit(solution)/shard_map/ppermute | solution.py:26
  65.6 0.8 %collective-permute-start.19 = (f32[128,256]{1,0:T(8,128)S(1)}, f32[128,256]{1,0:T(8,128)S(1)}, u32[]{:S(2)}, u32[]{:S(2)}) collective-permute-start(f32[128,256]{1,0:T(8,128)S(1)} %slice.259), channel_id=1, source_target_pairs={{0,4},{4,0},{1,5},{5,1},{2,6},{6,2},{3,7},{7,3},{8,12},{12,8},{9,1... | collective-permute-start | bytes 393224 | tf_op jit(solution)/shard_map/ppermute | solution.py:26
  66.5 2.0 %collective-permute-start.21 = (f32[128,128]{1,0:T(8,128)S(1)}, f32[128,128]{1,0:T(8,128)S(1)}, u32[]{:S(2)}, u32[]{:S(2)}) collective-permute-start(f32[128,128]{1,0:T(8,128)S(1)} %slice_add_fusion.2), channel_id=1, source_target_pairs={{0,16},{8,24},{16,0},{24,8},{1,17},{9,25},{17,1},{25,9},{2,18},{10... | collective-permute-start | bytes 196616 | tf_op jit(solution)/shard_map/ppermute | solution.py:26
  68.5 1.0 %collective-permute-start.23 = (f32[128,128]{1,0:T(8,128)S(1)}, f32[128,128]{1,0:T(8,128)S(1)}, u32[]{:S(2)}, u32[]{:S(2)}) collective-permute-start(f32[128,128]{1,0:T(8,128)S(1)} %slice_add_fusion.1), channel_id=1, source_target_pairs={{0,16},{8,24},{16,0},{24,8},{1,17},{9,25},{17,1},{25,9},{2,18},{10... | collective-permute-start | bytes 196616 | tf_op jit(solution)/shard_map/ppermute | solution.py:26
  69.6 1.5 %collective-permute-start.18 = (f32[128,256]{1,0:T(8,128)S(1)}, f32[128,256]{1,0:T(8,128)S(1)}, u32[]{:S(2)}, u32[]{:S(2)}) collective-permute-start(f32[128,256]{1,0:T(8,128)S(1)} %dynamic-slice_add_fusion), channel_id=1, source_target_pairs={{0,2},{1,3},{2,0},{3,1},{4,6},{5,7},{6,4},{7,5},{8,10},{9,11},{10,... | collective-permute-start | bytes 393224 | tf_op jit(solution)/shard_map/ppermute | solution.py:26
  71.1 0.7 maximum_select_fusion
  72.1 1.6 %collective-permute-done.23 = f32[128,128]{1,0:T(8,128)S(1)} collective-permute-done((f32[128,128]{1,0:T(8,128)S(1)}, f32[128,128]{1,0:T(8,128)S(1)}, u32[]{:S(2)}, u32[]{:S(2)}) %collective-permute-start.23) | collective-permute-done | bytes 65568 | tf_op jit(solution)/shard_map/ppermute | solution.py:26
  73.6 0.7 fusion.35
  74.6 0.7 add_add_fusion
  (113 shorter events, 7.5 us)
Async XLA Ops:
  0.6 5.7 %copy-start = (f32[1024,256]{1,0:T(8,128)S(1)}, f32[1024,256]{1,0:T(8,128)}, u32[]{:S(2)}) copy-start(f32[1024,256]{1,0:T(8,128)} %param.6) | copy-start | bytes 3145732
  0.6 12.2 %collective-permute-start = (f32[128,256]{1,0:T(8,128)}, f32[128,256]{1,0:T(8,128)S(1)}, u32[]{:S(2)}, u32[]{:S(2)}) collective-permute-start(f32[128,256]{1,0:T(8,128)} %param.7), channel_id=1, source_target_pairs={{0,16},{8,24},{16,0},{24,8},{1,17},{9,25},{17,1},{25,9},{2,18},{10... | collective-permute-start | bytes 393224 | tf_op jit(solution)/shard_map/ppermute | solution.py:26
  4.8 8.7 %collective-permute-start.1 = (f32[128,256]{1,0:T(8,128)}, f32[128,256]{1,0:T(8,128)S(1)}, u32[]{:S(2)}, u32[]{:S(2)}) collective-permute-start(f32[128,256]{1,0:T(8,128)} %param.7), channel_id=1, source_target_pairs={{0,4},{4,0},{1,5},{5,1},{2,6},{6,2},{3,7},{7,3},{8,12},{12,8},{9,1... | collective-permute-start | bytes 393224 | tf_op jit(solution)/shard_map/ppermute | solution.py:26
  6.3 3.8 %copy-start.1 = (f32[128,1024]{1,0:T(8,128)S(1)}, f32[128,1024]{1,0:T(8,128)}, u32[]{:S(2)}) copy-start(f32[128,1024]{1,0:T(8,128)} %param.5) | copy-start | bytes 1572868
  7.8 6.4 %collective-permute-start.2 = (f32[128,256]{1,0:T(8,128)S(1)}, f32[128,256]{1,0:T(8,128)S(1)}, u32[]{:S(2)}, u32[]{:S(2)}) collective-permute-start(f32[128,256]{1,0:T(8,128)S(1)} %get-tuple-element.65), channel_id=1, source_target_pairs={{0,8},{8,0},{16,24},{24,16},{1,9},{9,1},{17,25},{25,17},{2,10},{10... | collective-permute-start | bytes 393224 | tf_op jit(solution)/shard_map/ppermute | solution.py:26
  9.5 0.7 copy-start.9
  10.7 10.2 %collective-permute-start.12 = (f32[129,512]{1,0:T(8,128)S(1)}, f32[129,512]{1,0:T(8,128)S(1)}, u32[]{:S(2)}, u32[]{:S(2)}) collective-permute-start(f32[129,512]{1,0:T(8,128)S(1)} %pad_maximum_fusion.1), channel_id=1, source_target_pairs={{0,8},{8,0},{16,24},{24,16},{1,9},{9,1},{17,25},{25,17},{2,10},{10... | collective-permute-start | bytes 792584 | tf_op jit(solution)/shard_map/ppermute | solution.py:26
  11.3 0.9 %copy-start.2 = (f32[128,256]{1,0:T(8,128)S(1)}, f32[128,256]{1,0:T(8,128)}, u32[]{:S(2)}) copy-start(f32[128,256]{1,0:T(8,128)} %param.7) | copy-start | bytes 393220
  12.9 5.0 %collective-permute-start.5 = (f32[128,256]{1,0:T(8,128)S(1)}, f32[128,256]{1,0:T(8,128)S(1)}, u32[]{:S(2)}, u32[]{:S(2)}) collective-permute-start(f32[128,256]{1,0:T(8,128)S(1)} %collective-permute-done), channel_id=1, source_target_pairs={{0,4},{4,0},{1,5},{5,1},{2,6},{6,2},{3,7},{7,3},{8,12},{12,8},{9,1... | collective-permute-start | bytes 393224 | tf_op jit(solution)/shard_map/ppermute | solution.py:26
  14.6 10.5 %collective-permute-start.3 = (f32[192,256]{1,0:T(8,128)S(1)}, f32[192,256]{1,0:T(8,128)S(1)}, u32[]{:S(2)}, u32[]{:S(2)}) collective-permute-start(f32[192,256]{1,0:T(8,128)S(1)} %fusion.25), channel_id=1, source_target_pairs={{0,1},{1,0},{2,3},{3,2},{4,5},{5,4},{6,7},{7,6},{8,9},{9,8},{10,11... | collective-permute-start | bytes 589832 | tf_op jit(solution)/shard_map/ppermute | solution.py:26
  14.8 4.2 %copy-start.3 = (f32[256]{0:T(256)}, f32[256]{0:T(256)S(1)}, u32[]{:S(2)}) copy-start(f32[256]{0:T(256)S(1)} %multiply_reduce_fusion.2) | copy-start | bytes 3076
  19.0 0.5 copy-start.5
  19.0 0.6 copy-start.7
  20.9 1.5 %collective-permute-start.6 = (f32[72,256]{1,0:T(8,128)}, f32[72,256]{1,0:T(8,128)S(1)}, u32[]{:S(2)}, u32[]{:S(2)}) collective-permute-start(f32[72,256]{1,0:T(8,128)} %dynamic_update_slice.33), channel_id=1, source_target_pairs={{0,1},{1,0},{2,3},{3,2},{4,5},{5,4},{6,7},{7,6},{8,9},{9,8},{10,11... | collective-permute-start | bytes 221192 | tf_op jit(solution)/shard_map/ppermute | solution.py:26
  21.0 0.7 copy-start.10
  22.7 0.7 copy-start.4
  22.7 0.7 copy-start.6
  22.7 0.7 copy-start.8
  23.6 4.4 %collective-permute-start.7 = (f32[72,256]{1,0:T(8,128)S(1)}, f32[72,256]{1,0:T(8,128)S(1)}, u32[]{:S(2)}, u32[]{:S(2)}) collective-permute-start(f32[72,256]{1,0:T(8,128)S(1)} %dynamic_update_slice.35), channel_id=1, source_target_pairs={{0,2},{1,3},{2,0},{3,1},{4,6},{5,7},{6,4},{7,5},{8,10},{9,11},{10,... | collective-permute-start | bytes 221192 | tf_op jit(solution)/shard_map/ppermute | solution.py:26
  25.5 6.7 %collective-permute-start.4 = (f32[192,256]{1,0:T(8,128)S(1)}, f32[192,256]{1,0:T(8,128)S(1)}, u32[]{:S(2)}, u32[]{:S(2)}) collective-permute-start(f32[192,256]{1,0:T(8,128)S(1)} %convolution_add_fusion), channel_id=1, source_target_pairs={{0,2},{1,3},{2,0},{3,1},{4,6},{5,7},{6,4},{7,5},{8,10},{9,11},{10,... | collective-permute-start | bytes 589832 | tf_op jit(solution)/shard_map/ppermute | solution.py:26
  32.8 3.7 %collective-permute-start.10 = (f32[2,256]{1,0:T(2,128)S(1)}, f32[2,256]{1,0:T(2,128)S(1)}, u32[]{:S(2)}, u32[]{:S(2)}) collective-permute-start(f32[2,256]{1,0:T(2,128)S(1)} %pad_maximum_fusion.15), channel_id=1, source_target_pairs={{0,4},{4,0},{1,5},{5,1},{2,6},{6,2},{3,7},{7,3},{8,12},{12,8},{9,1... | collective-permute-start | bytes 6152 | tf_op jit(solution)/shard_map/ppermute | solution.py:26
  33.4 3.5 %collective-permute-start.8 = (f32[2,256]{1,0:T(2,128)S(1)}, f32[2,256]{1,0:T(2,128)S(1)}, u32[]{:S(2)}, u32[]{:S(2)}) collective-permute-start(f32[2,256]{1,0:T(2,128)S(1)} %pad_maximum_fusion.13), channel_id=1, source_target_pairs={{0,1},{1,0},{2,3},{3,2},{4,5},{5,4},{6,7},{7,6},{8,9},{9,8},{10,11... | collective-permute-start | bytes 6152 | tf_op jit(solution)/shard_map/ppermute | solution.py:26
  36.5 4.5 %collective-permute-start.11 = (f32[2,256]{1,0:T(2,128)S(1)}, f32[2,256]{1,0:T(2,128)S(1)}, u32[]{:S(2)}, u32[]{:S(2)}) collective-permute-start(f32[2,256]{1,0:T(2,128)S(1)} %pad_maximum_fusion.16), channel_id=1, source_target_pairs={{0,16},{8,24},{16,0},{24,8},{1,17},{9,25},{17,1},{25,9},{2,18},{10... | collective-permute-start | bytes 6152 | tf_op jit(solution)/shard_map/ppermute | solution.py:26
  36.9 4.3 %collective-permute-start.9 = (f32[2,256]{1,0:T(2,128)S(1)}, f32[2,256]{1,0:T(2,128)S(1)}, u32[]{:S(2)}, u32[]{:S(2)}) collective-permute-start(f32[2,256]{1,0:T(2,128)S(1)} %pad_maximum_fusion.14), channel_id=1, source_target_pairs={{0,8},{8,0},{16,24},{24,16},{1,9},{9,1},{17,25},{25,17},{2,10},{10... | collective-permute-start | bytes 6152 | tf_op jit(solution)/shard_map/ppermute | solution.py:26
  41.6 1.6 %collective-permute-start.13 = (f32[264,256]{1,0:T(8,128)S(1)}, f32[264,256]{1,0:T(8,128)S(1)}, u32[]{:S(2)}, u32[]{:S(2)}) collective-permute-start(f32[264,256]{1,0:T(8,128)S(1)} %constant_dynamic-update-slice_fusion), channel_id=1, source_target_pairs={{0,1},{1,0},{2,3},{3,2},{4,5},{5,4},{6,7},{7,6},{8,9},{9,8},{10,11... | collective-permute-start | bytes 811016 | tf_op jit(solution)/shard_map/ppermute | solution.py:26
  44.0 6.4 %collective-permute-start.14 = (f32[256,128]{1,0:T(8,128)S(1)}, f32[256,128]{1,0:T(8,128)S(1)}, u32[]{:S(2)}, u32[]{:S(2)}) collective-permute-start(f32[256,128]{1,0:T(8,128)S(1)} %fusion.7), channel_id=1, source_target_pairs={{0,8},{8,0},{16,24},{24,16},{1,9},{9,1},{17,25},{25,17},{2,10},{10... | collective-permute-start | bytes 393224 | tf_op jit(solution)/shard_map/ppermute | solution.py:26
  46.4 6.2 %collective-permute-start.15 = (f32[256,128]{1,0:T(8,128)S(1)}, f32[256,128]{1,0:T(8,128)S(1)}, u32[]{:S(2)}, u32[]{:S(2)}) collective-permute-start(f32[256,128]{1,0:T(8,128)S(1)} %fusion.4), channel_id=1, source_target_pairs={{0,8},{8,0},{16,24},{24,16},{1,9},{9,1},{17,25},{25,17},{2,10},{10... | collective-permute-start | bytes 393224 | tf_op jit(solution)/shard_map/ppermute | solution.py:26
  46.5 19.9 %collective-permute-start.24 = (f32[128,256]{1,0:T(8,128)S(1)}, f32[128,256]{1,0:T(8,128)S(1)}, u32[]{:S(2)}, u32[]{:S(2)}) collective-permute-start(f32[128,256]{1,0:T(8,128)S(1)} %pad_maximum_fusion.8), channel_id=1, source_target_pairs={{0,4},{4,0},{1,5},{5,1},{2,6},{6,2},{3,7},{7,3},{8,12},{12,8},{9,1... | collective-permute-start | bytes 393224 | tf_op jit(solution)/shard_map/ppermute | solution.py:26
  48.1 6.6 %collective-permute-start.25 = (f32[128,256]{1,0:T(8,128)S(1)}, f32[128,256]{1,0:T(8,128)S(1)}, u32[]{:S(2)}, u32[]{:S(2)}) collective-permute-start(f32[128,256]{1,0:T(8,128)S(1)} %pad_maximum_fusion.9), channel_id=1, source_target_pairs={{0,4},{4,0},{1,5},{5,1},{2,6},{6,2},{3,7},{7,3},{8,12},{12,8},{9,1... | collective-permute-start | bytes 393224 | tf_op jit(solution)/shard_map/ppermute | solution.py:26
  54.7 13.8 %collective-permute-start.26 = (f32[128,256]{1,0:T(8,128)S(1)}, f32[128,256]{1,0:T(8,128)S(1)}, u32[]{:S(2)}, u32[]{:S(2)}) collective-permute-start(f32[128,256]{1,0:T(8,128)S(1)} %maximum_add_fusion.1), channel_id=1, source_target_pairs={{0,16},{8,24},{16,0},{24,8},{1,17},{9,25},{17,1},{25,9},{2,18},{10... | collective-permute-start | bytes 393224 | tf_op jit(solution)/shard_map/ppermute | solution.py:26
  56.4 17.9 %collective-permute-start.16 = (f32[128,256]{1,0:T(8,128)S(1)}, f32[128,256]{1,0:T(8,128)S(1)}, u32[]{:S(2)}, u32[]{:S(2)}) collective-permute-start(f32[128,256]{1,0:T(8,128)S(1)} %get-tuple-element.28), channel_id=1, source_target_pairs={{0,1},{1,0},{2,3},{3,2},{4,5},{5,4},{6,7},{7,6},{8,9},{9,8},{10,11... | collective-permute-start | bytes 393224 | tf_op jit(solution)/shard_map/ppermute | solution.py:26
  56.5 13.0 %collective-permute-start.17 = (f32[128,256]{1,0:T(8,128)S(1)}, f32[128,256]{1,0:T(8,128)S(1)}, u32[]{:S(2)}, u32[]{:S(2)}) collective-permute-start(f32[128,256]{1,0:T(8,128)S(1)} %get-tuple-element.29), channel_id=1, source_target_pairs={{0,1},{1,0},{2,3},{3,2},{4,5},{5,4},{6,7},{7,6},{8,9},{9,8},{10,11... | collective-permute-start | bytes 393224 | tf_op jit(solution)/shard_map/ppermute | solution.py:26
  57.0 4.3 %collective-permute-start.20 = (f32[128,128]{1,0:T(8,128)S(1)}, f32[128,128]{1,0:T(8,128)S(1)}, u32[]{:S(2)}, u32[]{:S(2)}) collective-permute-start(f32[128,128]{1,0:T(8,128)S(1)} %slice.263), channel_id=1, source_target_pairs={{0,4},{4,0},{1,5},{5,1},{2,6},{6,2},{3,7},{7,3},{8,12},{12,8},{9,1... | collective-permute-start | bytes 196616 | tf_op jit(solution)/shard_map/ppermute | solution.py:26
  61.4 4.3 %collective-permute-start.22 = (f32[128,128]{1,0:T(8,128)S(1)}, f32[128,128]{1,0:T(8,128)S(1)}, u32[]{:S(2)}, u32[]{:S(2)}) collective-permute-start(f32[128,128]{1,0:T(8,128)S(1)} %slice.265), channel_id=1, source_target_pairs={{0,4},{4,0},{1,5},{5,1},{2,6},{6,2},{3,7},{7,3},{8,12},{12,8},{9,1... | collective-permute-start | bytes 196616 | tf_op jit(solution)/shard_map/ppermute | solution.py:26
  65.6 6.1 %collective-permute-start.19 = (f32[128,256]{1,0:T(8,128)S(1)}, f32[128,256]{1,0:T(8,128)S(1)}, u32[]{:S(2)}, u32[]{:S(2)}) collective-permute-start(f32[128,256]{1,0:T(8,128)S(1)} %slice.259), channel_id=1, source_target_pairs={{0,4},{4,0},{1,5},{5,1},{2,6},{6,2},{3,7},{7,3},{8,12},{12,8},{9,1... | collective-permute-start | bytes 393224 | tf_op jit(solution)/shard_map/ppermute | solution.py:26
  66.5 5.6 %collective-permute-start.21 = (f32[128,128]{1,0:T(8,128)S(1)}, f32[128,128]{1,0:T(8,128)S(1)}, u32[]{:S(2)}, u32[]{:S(2)}) collective-permute-start(f32[128,128]{1,0:T(8,128)S(1)} %slice_add_fusion.2), channel_id=1, source_target_pairs={{0,16},{8,24},{16,0},{24,8},{1,17},{9,25},{17,1},{25,9},{2,18},{10... | collective-permute-start | bytes 196616 | tf_op jit(solution)/shard_map/ppermute | solution.py:26
  68.5 5.2 %collective-permute-start.23 = (f32[128,128]{1,0:T(8,128)S(1)}, f32[128,128]{1,0:T(8,128)S(1)}, u32[]{:S(2)}, u32[]{:S(2)}) collective-permute-start(f32[128,128]{1,0:T(8,128)S(1)} %slice_add_fusion.1), channel_id=1, source_target_pairs={{0,16},{8,24},{16,0},{24,8},{1,17},{9,25},{17,1},{25,9},{2,18},{10... | collective-permute-start | bytes 196616 | tf_op jit(solution)/shard_map/ppermute | solution.py:26
  69.6 5.0 %collective-permute-start.18 = (f32[128,256]{1,0:T(8,128)S(1)}, f32[128,256]{1,0:T(8,128)S(1)}, u32[]{:S(2)}, u32[]{:S(2)}) collective-permute-start(f32[128,256]{1,0:T(8,128)S(1)} %dynamic-slice_add_fusion), channel_id=1, source_target_pairs={{0,2},{1,3},{2,0},{3,1},{4,6},{5,7},{6,4},{7,5},{8,10},{9,11},{10,... | collective-permute-start | bytes 393224 | tf_op jit(solution)/shard_map/ppermute | solution.py:26
